TPU v7x, 32 devices: a whole 2x2x4 slice. The times are simulated.
32 devices in a mesh: grp: 2 (over y), res: 4 (over z), seq: 2 (over x), head: 2 (over core).
Axes of the slice: x: 2, y: 2, z: 4, core: 2. Of those that a mesh axis runs over, the one named last changes fastest.
Arguments:
- tokens: bfloat16 [24, 512, 768], P(('grp', 'seq'), 'res'), parts along dimension 0, may hold values from -20 to 20
- weights: int32 [24], P(('grp', 'seq')), parts along dimension 0, may hold values from 3 to 17
- key_mask: int32 [1024], P(('grp', 'res')), parts along dimension 0, may hold values 0 or 1
- w_query: bfloat16 [768, 768], P(None, 'head'), may hold values from -0.21875 to 0.21875
- w_key: bfloat16 [768, 768], P(None, 'head'), may hold values from -0.21875 to 0.21875
- w_value: bfloat16 [768, 768], P(None, 'head'), may hold values from -0.21875 to 0.21875
- w_out: bfloat16 [768, 768], P('head'), may hold values from -0.21875 to 0.21875
Outputs:
- attention_out: bfloat16 [24, 512, 768], P(('grp', 'seq'), 'res', 'head'), parts along dimension 0
There are 2 independent parts, one for each index of `grp`. A program takes and returns all parts, laid end to end along the dimension named above; an argument that names none is the same for every part. Nothing has to cross between parts.
All inputs are finite; a program needn't handle non-finite values. No bound on the sum of `key_mask` on one device may be relied on, other than what follows from the above.
Results may differ from a plain program's by a relative error of at most 0.011.
The roundings to bfloat16 on the way count: a program that leaves them out, or rounds other values in their place, can miss the bound.
Values may be sent and summed in bfloat16 or wider, within the bound.
No kernel may reach another device: no remote copies, remote signals or barrier semaphores. Data moves between devices by JAX's collectives and lax.ppermute only.
A program may use at most 64 MiB of HBM per device.

v0:
```python
import functools
import math

import jax
import jax.numpy as jnp
from jax import lax
from jax.experimental import pallas as pl
from jax.experimental.pallas import tpu as pltpu
from jax.sharding import PartitionSpec as P


HEAD_DIM = 64
LANES = 128
PER_TILE = LANES // HEAD_DIM
CHUNKS = 2
MARK_ROWS = 8
PIECE = 32
PARTS = HEAD_DIM // PIECE
MASKED = -1000000000.0
VMEM_LIMIT = 24 * 1024 * 1024


def ring(value, axis, by=1):
    length = lax.axis_size(axis)
    return lax.ppermute(value, axis, [(i, (i + by) % length) for i in range(length)])


def whole(count):
    return [pl.BlockSpec(memory_space=pltpu.VMEM) for _ in range(count)]


def call(kernel, out_shape, args, flops, scalars=0, scratch=()):
    specs = [pl.BlockSpec(memory_space=pltpu.SMEM)] * scalars + whole(len(args) - scalars)
    multiple = isinstance(out_shape, (list, tuple))
    size = sum(a.size * a.dtype.itemsize for a in args)
    return pl.pallas_call(
        kernel,
        out_shape=out_shape,
        in_specs=specs,
        out_specs=whole(len(out_shape)) if multiple else whole(1)[0],
        scratch_shapes=list(scratch),
        cost_estimate=pl.CostEstimate(flops=int(flops), transcendentals=0, bytes_accessed=int(size)),
        compiler_params=pltpu.CompilerParams(vmem_limit_bytes=VMEM_LIMIT),
    )(*args)


def lane_head(shape):
    return lax.broadcasted_iota(jnp.int32, shape, len(shape) - 1) // HEAD_DIM


def dot(a, b):
    return jnp.dot(a, b, preferred_element_type=jnp.float32)


def dot_nt(a, b):
    return lax.dot_general(a, b, (((1,), (1,)), ((), ())), preferred_element_type=jnp.float32)


def tile_lanes(tile):
    return slice(tile * LANES, (tile + 1) * LANES)


def beside(flat, cells, tile):
    rows = flat.shape[0] // cells
    return jnp.concatenate(
        [flat[row * cells : (row + 1) * cells, tile_lanes(tile)] for row in range(rows)], axis=1
    )


def spread(target, chunk, flat, cells, first_row=0, first_cell=0):
    heads = lane_head((cells, LANES))
    for tile in range(flat.shape[1] // LANES):
        for row in range(flat.shape[0] // cells):
            part = flat[row * cells : (row + 1) * cells, tile_lanes(tile)]
            for h in range(PER_TILE):
                kept = jnp.where(heads == h, part, jnp.zeros_like(part))
                top = h * HEAD_DIM + first_cell
                target[chunk, tile, top : top + cells, tile_lanes(first_row + row)] = kept


def own_row(row, share, cores):
    core = lax.axis_index("head")
    return lax.rem(core + (cores - row // share), cores) * share + row % share


def live_rows(mask, first, count):
    cell = lax.broadcasted_iota(jnp.int32, (count, LANES), 0) + first
    here = cell == lax.broadcasted_iota(jnp.int32, (count, LANES), 1)
    marks = jnp.broadcast_to(mask[:1], (count, LANES))
    return jnp.max(jnp.where(here, marks, 0.0), axis=1, keepdims=True) > 0


def project(flat, w):
    return dot(flat, w[...]).astype(jnp.bfloat16)


def pack_kernel(tokens, mask, packed, landing, marks, done, *, chunk, share):
    _, part, width = landing.shape
    core = lax.axis_index("head")
    size = share * part
    used = width // LANES * size
    copies = [
        pltpu.make_async_copy(
            tokens.at[pl.ds(core * share, share), pl.ds(chunk * part, part)], landing, done.at[0]
        )
    ]
    if packed.shape[0] > used:
        copies.append(pltpu.make_async_copy(mask, marks, done.at[1]))
    for copy in copies:
        copy.start()
    for copy in copies:
        copy.wait()
    for tile in range(width // LANES):
        at = slice(tile * LANES, (tile + 1) * LANES)
        packed[tile * size : (tile + 1) * size] = landing[:, :, at].reshape(size, LANES)
    if packed.shape[0] > used:
        tail = packed.shape[0] - used
        packed[used:] = jnp.broadcast_to(marks[...].astype(jnp.float32), (tail, LANES)).astype(jnp.bfloat16)


def unpack(pieces, width):
    tiles = width // LANES
    flats = []
    for piece in pieces:
        size = piece.shape[0] // tiles // PIECE * PIECE
        flats.append(
            jnp.concatenate([piece[tile * size : (tile + 1) * size] for tile in range(tiles)], axis=1)
        )
    return jnp.concatenate(flats, axis=0)


def marks_of(piece):
    return piece[piece.shape[0] - MARK_ROWS :].astype(jnp.float32)


def project_kernel(query, w_key, w_value, *refs, order, masked):
    pieces, (logits, values) = refs[:-2], refs[-2:]
    per_chunk = len(pieces) // len(order)
    marks = marks_of(pieces[0])
    for at, chunk in enumerate(order):
        flat = unpack(pieces[at * per_chunk : (at + 1) * per_chunk], w_key.shape[0])
        keys = project(flat, w_key)
        live = live_rows(marks, chunk * HEAD_DIM, HEAD_DIM)
        for tile in range(query.shape[0]):
            total = dot_nt(beside(keys, HEAD_DIM, tile), query[tile])
            logits[tile, at * HEAD_DIM : (at + 1) * HEAD_DIM] = jnp.where(live, total, masked)
        spread(values, at, project(flat, w_value), HEAD_DIM)


def early_kernel(query, w_key, piece, logits):
    cells = logits.shape[1]
    keys = project(unpack([piece], w_key.shape[0]), w_key)
    width = keys.shape[0] // cells * LANES
    for tile in range(query.shape[0]):
        logits[tile] = dot_nt(beside(keys, cells, tile), query[tile, :, :width])


def late_kernel(query, w_key, marks, before, *refs, first, masked):
    pieces, logits = refs[:-1], refs[-1]
    cells = logits.shape[1]
    keys = project(unpack(pieces, w_key.shape[0]), w_key)
    live = live_rows(marks_of(marks), first, cells)
    skip = query.shape[2] - keys.shape[0] // cells * LANES
    for tile in range(query.shape[0]):
        total = before[tile] + dot_nt(beside(keys, cells, tile), query[tile, :, skip:])
        logits[tile] = jnp.where(live, total, masked)


def values_kernel(w_value, *refs, parts):
    pieces, values = refs[:-1], refs[-1]
    per_part = len(pieces) // parts
    cells = HEAD_DIM // parts
    for at in range(parts):
        flat = unpack(pieces[at * per_part : (at + 1) * per_part], w_value.shape[0])
        spread(values, 0, project(flat, w_value), cells, 0, at * cells)


def split_kernel(packed, *parts, tiles):
    size = packed.shape[0] // tiles
    count = len(parts)
    for at, part in enumerate(parts):
        for block in range(tiles * size // PIECE // count):
            source = (block * count + at) * PIECE
            part[block * PIECE : (block + 1) * PIECE] = packed[source : source + PIECE]


def own_kernel(*refs, cores, masked):
    counts, refs = refs[:-9], refs[-9:]
    mask, tokens, w_query, w_key, w_value, query, logits, values, keys = refs
    rows, cells, width = tokens.shape
    share = rows // cores
    tiles = query.shape[0]
    total = sum(count[row] for count in counts for row in range(rows))
    scale = lax.rsqrt(jnp.full((1, tiles * LANES), total, jnp.int32).astype(jnp.float32))
    heads = lane_head((cells, LANES))
    for part in range(cores):
        start = own_row(part * share, share, cores)
        block = tokens[pl.ds(start, share)].reshape(share * cells, width)
        asked = dot(block, w_query[...])
        key = project(block, w_key)
        value = project(block, w_value)
        for near in range(share):
            row = part * share + near
            at = slice(near * cells, (near + 1) * cells)
            count = jnp.full(scale.shape, counts[0][start + near], jnp.int32).astype(jnp.float32)
            factor = count * scale / math.sqrt(HEAD_DIM)
            scaled = (asked[at] * factor).astype(jnp.bfloat16)
            for tile in range(tiles):
                own = scaled[:, tile_lanes(tile)]
                keys[tile, :, tile_lanes(row)] = key[at, tile_lanes(tile)]
                for h in range(PER_TILE):
                    kept = jnp.where(heads == h, own, jnp.zeros_like(own))
                    query[tile, h * cells : (h + 1) * cells, tile_lanes(row)] = kept
            for chunk in range(CHUNKS):
                spread(values, chunk, value[at][chunk * HEAD_DIM : (chunk + 1) * HEAD_DIM], HEAD_DIM, row)
    live = live_rows(mask[...].astype(jnp.float32), 0, cells)
    for tile in range(tiles):
        logits[tile] = jnp.where(live, dot_nt(keys[tile], query[tile]), masked)


def upright(lines):
    return jnp.concatenate([jnp.broadcast_to(line, (HEAD_DIM, LANES)) for line in lines], axis=0).T


def absorb(units, state, tile, rows):
    scores, mixed = [[] for _ in range(PER_TILE)], []
    for pieces, values in units:
        totals = []
        for shared in pieces:
            total = shared[0][tile]
            for other in shared[1:]:
                total = total + other[tile]
            totals.append(total)
        total = jnp.concatenate(totals, axis=0) if len(totals) > 1 else totals[0]
        for chunk in range(values.shape[0]):
            for h in range(PER_TILE):
                scores[h].append(total[chunk * HEAD_DIM : (chunk + 1) * HEAD_DIM, tile_lanes(h)])
            mixed.append(values[chunk, tile])
    tops, denoms, expos, rescales = [], [], [], []
    for h in range(PER_TILE):
        top = jnp.max(functools.reduce(jnp.maximum, scores[h]), axis=0, keepdims=True)
        if state is not None:
            before = state[0][tile, h * 8 : h * 8 + 1]
            top = jnp.maximum(top, before)
            rescales.append(jnp.exp(before - top))
        expo = [jnp.exp(score - top) for score in scores[h]]
        denom = jnp.sum(functools.reduce(jnp.add, expo), axis=0, keepdims=True)
        if state is not None:
            denom = denom + state[1][tile, h * 8 : h * 8 + 1] * rescales[h]
        tops.append(top)
        denoms.append(denom)
        expos.append(expo)
    probs = []
    for chunk in range(len(mixed)):
        together = jnp.concatenate([expos[h][chunk] for h in range(PER_TILE)], axis=0)
        probs.append(together.T.astype(jnp.bfloat16))
    accum = dot(jnp.concatenate(probs, axis=1), jnp.concatenate(mixed, axis=0))
    if state is not None:
        accum = accum + state[2][tile] * jnp.concatenate([upright(rescales)] * rows, axis=1)
    return tops, denoms, accum


def read_units(refs, sizes):
    units, at = [], 0
    for parts, size in sizes:
        pieces = [refs[at + n * size : at + (n + 1) * size] for n in range(parts)]
        at += parts * size
        units.append((pieces, refs[at]))
        at += 1
    return units, refs[at:]


def absorb_kernel(*refs, sizes, carried):
    units, refs = read_units(refs, sizes)
    state = refs[:3] if carried else None
    top, denom, accum = refs[-3:]
    rows = accum.shape[2] // LANES
    for tile in range(accum.shape[0]):
        tops, denoms, accum[tile] = absorb(units, state, tile, rows)
        for h in range(PER_TILE):
            top[tile, h * 8 : h * 8 + 8] = jnp.broadcast_to(tops[h], (8, LANES))
            denom[tile, h * 8 : h * 8 + 8] = jnp.broadcast_to(denoms[h], (8, LANES))


def columns_of(w_out, ahead, cores):
    columns = w_out.shape[1] // cores
    at = lax.rem(lax.axis_index("head") + ahead, cores) * columns
    return w_out[:, pl.ds(pl.multiple_of(at, LANES), columns)]


def finish_kernel(*refs, sizes, carried, cores):
    units, refs = read_units(refs, sizes)
    state = refs[:3] if carried else None
    w_out, attended, sent = refs[-3:]
    rows, _, _ = attended.shape
    for tile in range(attended.shape[2] // LANES):
        _, denoms, accum = absorb(units, state, tile, rows)
        inverse = upright([1.0 / denom for denom in denoms])
        for row in range(rows):
            part = accum[:, tile_lanes(row)] * inverse
            attended[row, :, tile_lanes(tile)] = part.astype(jnp.bfloat16)
    write_output(attended, columns_of(w_out, 1 % cores, cores), sent, cores)


def write_output(attended, w, target, cores):
    rows, cells, inner = attended.shape
    share = rows // cores
    for part in range(cores):
        block = attended[part * share : (part + 1) * share].reshape(share * cells, inner)
        out = dot(block, w).astype(target.dtype).reshape(share, cells, w.shape[1])
        target[pl.ds(own_row(part * share, share, cores), share)] = out


def output_kernel(attended, w_out, kept, *, ahead, cores):
    write_output(attended, columns_of(w_out, ahead, cores), kept, cores)


def batches(blocks):
    every = tuple(range(CHUNKS))
    out = []
    for step in range(1, blocks):
        if step < blocks - 3:
            out.append((step, every))
        else:
            out += [(step, (k,)) for k in every if (step, k) != (blocks - 1, CHUNKS - 1)]
    return out


def shards(tokens, weights, key_mask, w_query, w_key, w_value, w_out):
    rows, cells, width = tokens.shape
    inner = w_query.shape[1]
    tiles = inner // LANES
    blocks = lax.axis_size("res")
    holders = lax.axis_size("seq")
    cores = lax.axis_size("head")
    part = HEAD_DIM
    share = rows // cores
    assert share * cores == rows and tiles * LANES == inner and part * CHUNKS == cells == LANES
    f32, bf16 = jnp.float32, jnp.bfloat16
    masked = MASKED / holders
    shape = pltpu.VMEM
    key_mask = key_mask.reshape(1, cells)

    length = share * part * width // LANES
    hbm = pl.BlockSpec(memory_space=pltpu.HBM)
    moving = [
        pl.pallas_call(
            functools.partial(pack_kernel, chunk=k, share=share),
            out_shape=shape((length + (0 if k else MARK_ROWS), LANES), bf16),
            in_specs=[hbm, hbm],
            out_specs=whole(1)[0],
            scratch_shapes=[
                shape((share, part, width), bf16),
                shape((1, cells), jnp.int32),
                pltpu.SemaphoreType.DMA((2,)),
            ],
            compiler_params=pltpu.CompilerParams(vmem_limit_bytes=VMEM_LIMIT),
        )(pltpu.with_memory_space_constraint(tokens, pltpu.HBM), pltpu.with_memory_space_constraint(key_mask, pltpu.HBM))
        for k in range(CHUNKS)
    ]
    counts = [weights]
    for k in range(1, holders):
        counts.append(ring(weights, "seq", k))

    def exchange(logits):
        return [logits] + [ring(logits, "seq", k) for k in range(1, holders)]

    depth = PER_TILE * part
    spans = rows * LANES
    query, logits, values = call(
        functools.partial(own_kernel, cores=cores, masked=masked),
        [
            shape((tiles, PER_TILE * cells, spans), bf16),
            shape((tiles, cells, PER_TILE * cells), f32),
            shape((CHUNKS, tiles, depth, spans), bf16),
        ],
        counts + [key_mask, tokens, w_query, w_key, w_value],
        2 * rows * cells * inner * (3 * width + cells * PER_TILE),
        holders,
        [shape((tiles, cells, spans), bf16)],
    )
    units = [([exchange(logits)], values)]

    pieces, moved = {}, {}

    def shared_rows(value):
        return [value] + [ring(value, "head", j) for j in range(1, cores)]

    last, tail = blocks - 1, CHUNKS - 1
    fine = []
    for step in range(1, blocks):
        if step == last:
            size = moving[tail].shape[0] // (PARTS * PIECE) * PIECE
            fine = call(
                functools.partial(split_kernel, tiles=width // LANES),
                [shape((size, LANES), bf16) for _ in range(PARTS)],
                [moving[tail]],
                0,
            )
            fine = [ring(fine[n], "res") for n in range(PARTS)]
        count = tail if step == last else CHUNKS
        moving = [ring(moving[k], "res") for k in range(count)]
        moved[step] = moving[0]
        for k in range(count):
            pieces[step, k] = shared_rows(moving[k])

    def kernel(function, outs, args, work):
        return call(function, outs, args, 2 * part * inner * work)

    def logits_shape(count):
        return shape((tiles, count, PER_TILE * cells), f32)

    def values_shape(count):
        return shape((count, tiles, depth, spans), bf16)

    def score_of(mine, marks, first, count):
        early = kernel(early_kernel, logits_shape(count), [query, w_key, mine[0]], width * share)
        late = functools.partial(late_kernel, first=first, masked=masked)
        args = [query, w_key, marks, early] + mine[1:]
        return exchange(kernel(late, logits_shape(count), args, width * share))

    def values_of(parts):
        function = functools.partial(values_kernel, parts=len(parts))
        return kernel(function, values_shape(1), [w_value] + sum(parts, []), width * rows)

    for step, taken in batches(blocks):
        count = len(taken)
        if count > 1 or cores == 1:
            outs = [logits_shape(count * part), values_shape(count)]
            args = [query, w_key, w_value] + sum([pieces[step, k] for k in taken], [])
            function = functools.partial(project_kernel, order=taken, masked=masked)
            logits, values = kernel(function, outs, args, 2 * count * width * rows)
            units.append(([exchange(logits)], values))
            continue
        mine = pieces[step, taken[0]]
        shared = score_of(mine, moved[step], taken[0] * part, part)
        units.append(([shared], values_of([mine])))

    tall = []
    for n, piece in enumerate(fine):
        mine = shared_rows(piece)
        tall.append((score_of(mine, moved[last], tail * part + n * PIECE, PIECE), mine))
    if tall:
        values = values_of([mine for _, mine in tall])
        units.append(([shared for shared, _ in tall], values))

    state = []
    state_shape = [
        shape((tiles, PER_TILE * 8, LANES), f32),
        shape((tiles, PER_TILE * 8, LANES), f32),
        shape((tiles, cells, spans), f32),
    ]

    def flatten(group):
        return sum([sum([list(piece) for piece in u[0]], []) + [u[1]] for u in group], [])

    def work(group):
        return sum(2 * cells * u[1].size for u in group)

    def sizes_of(group):
        return [(len(u[0]), len(u[0][0])) for u in group]

    cuts = groups_of(len(units))
    for cut in cuts[:-1]:
        group = units[slice(*cut)]
        state = call(
            functools.partial(absorb_kernel, sizes=sizes_of(group), carried=bool(state)),
            state_shape,
            flatten(group) + list(state),
            work(group),
        )
    group = units[slice(*cuts[-1])]
    columns = width // cores
    attended, sent = call(
        functools.partial(
            finish_kernel, sizes=sizes_of(group), carried=bool(state), cores=cores
        ),
        [shape((rows, cells, inner), bf16), shape((rows, cells, columns), bf16)],
        flatten(group) + list(state) + [w_out],
        work(group) + 2 * rows * cells * inner * columns,
    )

    def output(k):
        return call(
            functools.partial(output_kernel, ahead=k, cores=cores),
            shape((rows, cells, columns), f32),
            [attended, w_out],
            2 * rows * cells * inner * columns,
        )

    if cores == 1:
        return sent
    received = [ring(sent, "head")]
    for k in range(2, cores):
        received.append(ring(output(k).astype(bf16), "head", k))
    result = output(0)
    for value in received:
        result = result + value.astype(f32)
    return result.astype(bf16)


def groups_of(count):
    return [(at, min(at + 3, count - 1)) for at in range(0, count - 1, 3)] + [(count - 1, count)]


def solution(mesh):
    in_specs = (
        P(("grp", "seq"), "res", None),
        P(("grp", "seq")),
        P(("grp", "res")),
        P(None, "head"),
        P(None, "head"),
        P(None, "head"),
        P("head", None),
    )
    out_specs = P(("grp", "seq"), "res", "head")

    return jax.shard_map(shards, mesh=mesh, in_specs=in_specs, out_specs=out_specs, check_vma=False)
```

profile of v0, /device:TPU:0, one launch (start us, length us, event | category | flops | bytes accessed | tf_op | source)
XLA Modules:
  0.0 78.7 jit_solution(2551164957627771469)
XLA Ops:
  0.0 1.1 %shard_map.74 = bf16[1160,128]{1,0:T(8,128)(2,1)S(1)} custom-call(bf16[6,128,768]{2,1,0:T(8,128)(2,1)} %tokens.3, s32[1,128]{1,0:T(1,128)} %bitcast.1), custom_call_target="tpu_custom_call" | custom-call | tf_op jit(solution)/shard_map/pallas_call | solution.py:347
  1.1 0.0 copy-start
  1.2 0.0 copy-start.1
  1.2 0.0 copy-start.4
  1.2 0.0 copy-start.5
  1.2 3.1 %collective-permute-start.1 = (bf16[1160,128]{1,0:T(8,128)(2,1)S(1)}, bf16[1160,128]{1,0:T(8,128)(2,1)S(1)}, u32[]{:S(2)}, u32[]{:S(2)}) collective-permute-start(bf16[1160,128]{1,0:T(8,128)(2,1)S(1)} %shard_map.74), channel_id=1, source_target_pairs={{0,4},{4,8},{8,12},{12,0},{1,5},{5,9},{9,13},{13,1},{2,6},{6,10},{... | collective-permute-start | bytes 890888 | tf_op jit(solution)/shard_map/ppermute | solution.py:25
  4.3 1.0 %shard_map.75 = bf16[1152,128]{1,0:T(8,128)(2,1)S(1)} custom-call(bf16[6,128,768]{2,1,0:T(8,128)(2,1)} %tokens.3, s32[1,128]{1,0:T(1,128)} %bitcast.2), custom_call_target="tpu_custom_call" | custom-call | tf_op jit(solution)/shard_map/pallas_call | solution.py:347
  5.3 1.6 %collective-permute-start.4 = (bf16[1152,128]{1,0:T(8,128)(2,1)S(1)}, bf16[1152,128]{1,0:T(8,128)(2,1)S(1)}, u32[]{:S(2)}, u32[]{:S(2)}) collective-permute-start(bf16[1152,128]{1,0:T(8,128)(2,1)S(1)} %shard_map.75), channel_id=1, source_target_pairs={{0,4},{4,8},{8,12},{12,0},{1,5},{5,9},{9,13},{13,1},{2,6},{6,10},{... | collective-permute-start | bytes 884744 | tf_op jit(solution)/shard_map/ppermute | solution.py:25
  7.0 7.3 %collective-permute-done.1.piece.marks.refs_0_ = bf16[1160,128]{1,0:T(8,128)(2,1)S(1)} collective-permute-done((bf16[1160,128]{1,0:T(8,128)(2,1)S(1)}, bf16[1160,128]{1,0:T(8,128)(2,1)S(1)}, u32[]{:S(2)}, u32[]{:S(2)}) %collective-permute-start.1) | collective-permute-done | bytes 296992 | tf_op jit(solution)/shard_map/ppermute | solution.py:25
  14.2 6.3 %collective-permute-done.4.piece.refs_0_ = bf16[1152,128]{1,0:T(8,128)(2,1)S(1)} collective-permute-done((bf16[1152,128]{1,0:T(8,128)(2,1)S(1)}, bf16[1152,128]{1,0:T(8,128)(2,1)S(1)}, u32[]{:S(2)}, u32[]{:S(2)}) %collective-permute-start.4) | collective-permute-done | bytes 294944 | tf_op jit(solution)/shard_map/ppermute | solution.py:25
  20.5 0.0 collective-permute-start.21
  20.6 0.5 collective-permute-start.19
  21.1 5.8 %collective-permute-done.2.piece.marks.refs_0_ = bf16[1160,128]{1,0:T(8,128)(2,1)S(1)} collective-permute-done((bf16[1160,128]{1,0:T(8,128)(2,1)S(1)}, bf16[1160,128]{1,0:T(8,128)(2,1)S(1)}, u32[]{:S(2)}, u32[]{:S(2)}) %collective-permute-start.2) | collective-permute-done | bytes 296992 | tf_op jit(solution)/shard_map/ppermute | solution.py:25
  26.9 1.7 %collective-permute-start = (s32[6]{0:T(128)S(1)}, s32[6]{0:T(128)S(1)}, u32[]{:S(2)}, u32[]{:S(2)}) collective-permute-start(s32[6]{0:T(128)S(1)} %copy-done.6), channel_id=1, source_target_pairs={{0,2},{2,0},{1,3},{3,1},{4,6},{6,4},{5,7},{7,5},{8,10},{10,8},{9,1... | collective-permute-start | bytes 80 | tf_op jit(solution)/shard_map/ppermute | solution.py:25
  28.6 4.6 %collective-permute-done.5.packed.piece.refs_0_ = bf16[1152,128]{1,0:T(8,128)(2,1)S(1)} collective-permute-done((bf16[1152,128]{1,0:T(8,128)(2,1)S(1)}, bf16[1152,128]{1,0:T(8,128)(2,1)S(1)}, u32[]{:S(2)}, u32[]{:S(2)}) %collective-permute-start.5) | collective-permute-done | bytes 294944 | tf_op jit(solution)/shard_map/ppermute | solution.py:25
  33.3 0.1 collective-permute-start.9
  33.3 0.1 collective-permute-start.14
  33.5 2.9 %shard_map.73 = (bf16[3,256,768]{2,1,0:T(8,128)(2,1)S(1)}, f32[3,128,256]{2,1,0:T(8,128)S(1)}, bf16[2,3,128,768]{3,2,1,0:T(8,128)(2,1)S(1)}) custom-call(s32[6]{0:T(128)S(1)} %copy-done.6, s32[6]{0:T(128)S(1)} %collective-permute-done.refs_1_, s32[1,128]{1,0:T(1,128)S(1)} %bitcast.3, bf16[6,128,768]{2,1,0:T(8,128)(2,1)S(1)} %copy-done.2, ...), custom_call_target="tpu_custom_call" | custom-call | flops 1509949440 | bytes 2949680 | tf_op jit(solution)/shard_map/pallas_call | solution.py:36
  36.4 1.8 %collective-permute-start.18 = (f32[3,128,256]{2,1,0:T(8,128)S(1)}, f32[3,128,256]{2,1,0:T(8,128)S(1)}, u32[]{:S(2)}, u32[]{:S(2)}) collective-permute-start(f32[3,128,256]{2,1,0:T(8,128)S(1)} %get-tuple-element.21.refs_0_), channel_id=1, source_target_pairs={{0,2},{2,0},{1,3},{3,1},{4,6},{6,4},{5,7},{7,5},{8,10},{10,8},{9,1... | collective-permute-start | bytes 1179656 | tf_op jit(solution)/shard_map/ppermute | solution.py:25
  38.2 0.2 collective-permute-start.12
  38.4 1.2 %collective-permute-done.3.marks.piece.refs_0_ = bf16[1160,128]{1,0:T(8,128)(2,1)S(1)} collective-permute-done((bf16[1160,128]{1,0:T(8,128)(2,1)S(1)}, bf16[1160,128]{1,0:T(8,128)(2,1)S(1)}, u32[]{:S(2)}, u32[]{:S(2)}) %collective-permute-start.3) | collective-permute-done | bytes 296992 | tf_op jit(solution)/shard_map/ppermute | solution.py:25
  39.6 2.3 %collective-permute-done.9.piece.refs_2_ = bf16[576,128]{1,0:T(8,128)(2,1)S(1)} collective-permute-done((bf16[576,128]{1,0:T(8,128)(2,1)S(1)}, bf16[576,128]{1,0:T(8,128)(2,1)S(1)}, u32[]{:S(2)}, u32[]{:S(2)}) %collective-permute-start.9) | collective-permute-done | bytes 147488 | tf_op jit(solution)/shard_map/ppermute | solution.py:25
  41.9 0.0 collective-permute-start.6
  41.9 0.6 shard_map.94.before
  42.5 0.6 shard_map.91.before
  43.1 0.6 shard_map.95.refs_6_
  43.7 0.6 shard_map.92.refs_3_
  44.2 4.6 %collective-permute-done.6.piece.refs_0_ = bf16[576,128]{1,0:T(8,128)(2,1)S(1)} collective-permute-done((bf16[576,128]{1,0:T(8,128)(2,1)S(1)}, bf16[576,128]{1,0:T(8,128)(2,1)S(1)}, u32[]{:S(2)}, u32[]{:S(2)}) %collective-permute-start.6) | collective-permute-done | bytes 147488 | tf_op jit(solution)/shard_map/ppermute | solution.py:25
  48.8 1.5 %collective-permute-start.22 = (f32[3,64,256]{2,1,0:T(8,128)S(1)}, f32[3,64,256]{2,1,0:T(8,128)S(1)}, u32[]{:S(2)}, u32[]{:S(2)}) collective-permute-start(f32[3,64,256]{2,1,0:T(8,128)S(1)} %shard_map.95.refs_6_), channel_id=1, source_target_pairs={{0,2},{2,0},{1,3},{3,1},{4,6},{6,4},{5,7},{7,5},{8,10},{10,8},{9,1... | collective-permute-start | bytes 589832 | tf_op jit(solution)/shard_map/ppermute | solution.py:25
  50.3 0.5 collective-permute-start.20
  50.9 0.6 shard_map.85.before
  51.5 0.6 collective-permute-start.7
  52.0 0.6 shard_map.82.before
  52.6 0.6 shard_map.86.refs_3_
  53.2 0.6 shard_map.88.before
  53.8 0.6 shard_map.83.refs_0_
  54.4 0.6 shard_map.89.refs_6_
  55.0 1.6 %collective-permute-start.15 = (f32[3,64,256]{2,1,0:T(8,128)S(1)}, f32[3,64,256]{2,1,0:T(8,128)S(1)}, u32[]{:S(2)}, u32[]{:S(2)}) collective-permute-start(f32[3,64,256]{2,1,0:T(8,128)S(1)} %shard_map.86.refs_3_), channel_id=1, source_target_pairs={{0,2},{2,0},{1,3},{3,1},{4,6},{6,4},{5,7},{7,5},{8,10},{10,8},{9,1... | collective-permute-start | bytes 589832 | tf_op jit(solution)/shard_map/ppermute | solution.py:25
  56.5 0.6 collective-permute-start.13
  57.1 1.2 %collective-permute-done.20.refs_4_ = f32[3,64,256]{2,1,0:T(8,128)S(1)} collective-permute-done((f32[3,64,256]{2,1,0:T(8,128)S(1)}, f32[3,64,256]{2,1,0:T(8,128)S(1)}, u32[]{:S(2)}, u32[]{:S(2)}) %collective-permute-start.20) | collective-permute-done | bytes 196640 | tf_op jit(solution)/shard_map/ppermute | solution.py:25
  58.3 1.1 %collective-permute-start.17 = (f32[3,64,256]{2,1,0:T(8,128)S(1)}, f32[3,64,256]{2,1,0:T(8,128)S(1)}, u32[]{:S(2)}, u32[]{:S(2)}) collective-permute-start(f32[3,64,256]{2,1,0:T(8,128)S(1)} %shard_map.89.refs_6_), channel_id=1, source_target_pairs={{0,2},{2,0},{1,3},{3,1},{4,6},{6,4},{5,7},{7,5},{8,10},{10,8},{9,1... | collective-permute-start | bytes 589832 | tf_op jit(solution)/shard_map/ppermute | solution.py:25
  59.4 0.5 shard_map.96.refs_8_
  59.8 0.5 shard_map.93.refs_5_
  60.3 0.5 shard_map.79.before
  60.8 0.5 shard_map.77.before
  61.3 0.6 shard_map.97
  61.9 0.5 shard_map.80.refs_2_
  62.4 1.0 %collective-permute-start.11 = (f32[3,32,256]{2,1,0:T(8,128)S(1)}, f32[3,32,256]{2,1,0:T(8,128)S(1)}, u32[]{:S(2)}, u32[]{:S(2)}) collective-permute-start(f32[3,32,256]{2,1,0:T(8,128)S(1)} %shard_map.80.refs_2_), channel_id=1, source_target_pairs={{0,2},{2,0},{1,3},{3,1},{4,6},{6,4},{5,7},{7,5},{8,10},{10,8},{9,1... | collective-permute-start | bytes 294920 | tf_op jit(solution)/shard_map/ppermute | solution.py:25
  63.4 0.5 shard_map.78.refs_0_
  63.9 1.1 %collective-permute-start.8 = (f32[3,32,256]{2,1,0:T(8,128)S(1)}, f32[3,32,256]{2,1,0:T(8,128)S(1)}, u32[]{:S(2)}, u32[]{:S(2)}) collective-permute-start(f32[3,32,256]{2,1,0:T(8,128)S(1)} %shard_map.78.refs_0_), channel_id=1, source_target_pairs={{0,2},{2,0},{1,3},{3,1},{4,6},{6,4},{5,7},{7,5},{8,10},{10,8},{9,1... | collective-permute-start | bytes 294920 | tf_op jit(solution)/shard_map/ppermute | solution.py:25
  65.0 0.5 shard_map.87.refs_5_
  65.5 0.5 shard_map.81.refs_4_
  66.0 0.5 shard_map.84.refs_2_
  66.5 0.5 shard_map.90.refs_8_
  67.0 0.0 collective-permute-done.13.refs_1_
  67.0 4.2 %collective-permute-done.17.refs_7_ = f32[3,64,256]{2,1,0:T(8,128)S(1)} collective-permute-done((f32[3,64,256]{2,1,0:T(8,128)S(1)}, f32[3,64,256]{2,1,0:T(8,128)S(1)}, u32[]{:S(2)}, u32[]{:S(2)}) %collective-permute-start.17) | collective-permute-done | bytes 196640 | tf_op jit(solution)/shard_map/ppermute | solution.py:25
  71.2 0.6 shard_map.98
  71.8 1.5 %collective-permute-done.11.refs_3_ = f32[3,32,256]{2,1,0:T(8,128)S(1)} collective-permute-done((f32[3,32,256]{2,1,0:T(8,128)S(1)}, f32[3,32,256]{2,1,0:T(8,128)S(1)}, u32[]{:S(2)}, u32[]{:S(2)}) %collective-permute-start.11) | collective-permute-done | bytes 98336 | tf_op jit(solution)/shard_map/ppermute | solution.py:25
  73.3 1.5 %collective-permute-done.8.refs_1_ = f32[3,32,256]{2,1,0:T(8,128)S(1)} collective-permute-done((f32[3,32,256]{2,1,0:T(8,128)S(1)}, f32[3,32,256]{2,1,0:T(8,128)S(1)}, u32[]{:S(2)}, u32[]{:S(2)}) %collective-permute-start.8) | collective-permute-done | bytes 98336 | tf_op jit(solution)/shard_map/ppermute | solution.py:25
  74.8 0.9 %shard_map.99 = (bf16[6,128,384]{2,1,0:T(8,128)(2,1)S(1)}, bf16[6,128,384]{2,1,0:T(8,128)(2,1)S(1)}) custom-call(f32[3,32,256]{2,1,0:T(8,128)S(1)} %shard_map.78.refs_0_, f32[3,32,256]{2,1,0:T(8,128)S(1)} %collective-permute-done.8.refs_1_, f32[3,32,256]{2,1,0:T(8,128)S(1)} %shard_map.80.refs_2_, f32[3,32,256]{2,1,0:T(8,128)S(1)} %collective-permute-done.11.refs_3_, ...), custom_call_target="tpu_custom_call" | custom-call | flops 301989888 | bytes 2801664 | tf_op jit(solution)/shard_map/pallas_call | solution.py:36
  75.7 0.1 collective-permute-start.23
  75.8 0.5 shard_map.100
  76.3 1.4 %collective-permute-done.23 = bf16[6,128,384]{2,1,0:T(8,128)(2,1)S(1)} collective-permute-done((bf16[6,128,384]{2,1,0:T(8,128)(2,1)S(1)}, bf16[6,128,384]{2,1,0:T(8,128)(2,1)S(1)}, u32[]{:S(2)}, u32[]{:S(2)}) %collective-permute-start.23) | collective-permute-done | bytes 589856 | tf_op jit(solution)/shard_map/ppermute | solution.py:25
  77.8 1.0 %add_convert_fusion = bf16[6,128,384]{2,1,0:T(8,128)(2,1)} fusion(f32[6,128,384]{2,1,0:T(8,128)S(1)} %shard_map.100, bf16[6,128,384]{2,1,0:T(8,128)(2,1)S(1)} %collective-permute-done.23), kind=kLoop, calls=%fused_computation | loop fusion | flops 884736 | bytes 2359296 | tf_op jit(solution)/shard_map/convert_element_type | solution.py:499
  (27 shorter events, 0.1 us)
Async XLA Ops:
  0.0 26.9 %copy-start.6 = (s32[6]{0:T(128)S(1)}, s32[6]{0:T(128)}, u32[]{:S(2)}) copy-start(s32[6]{0:T(128)} %refs_0_.1) | copy-start | bytes 76
  0.0 33.4 %copy-start.2 = (bf16[6,128,768]{2,1,0:T(8,128)(2,1)S(1)}, bf16[6,128,768]{2,1,0:T(8,128)(2,1)}, u32[]{:S(2)}) copy-start(bf16[6,128,768]{2,1,0:T(8,128)(2,1)} %tokens.3) | copy-start | bytes 3538948
  1.1 32.3 %copy-start = (bf16[768,384]{1,0:T(8,128)(2,1)S(1)}, bf16[768,384]{1,0:T(8,128)(2,1)}, u32[]{:S(2)}) copy-start(bf16[768,384]{1,0:T(8,128)(2,1)} %w_key.27) | copy-start | bytes 1769476
  1.2 32.3 %copy-start.1 = (bf16[768,384]{1,0:T(8,128)(2,1)S(1)}, bf16[768,384]{1,0:T(8,128)(2,1)}, u32[]{:S(2)}) copy-start(bf16[768,384]{1,0:T(8,128)(2,1)} %w_value.11) | copy-start | bytes 1769476
  1.2 32.3 %copy-start.4 = (s32[128]{0:T(128)S(1)}, s32[128]{0:T(128)}, u32[]{:S(2)}) copy-start(s32[128]{0:T(128)} %param.9) | copy-start | bytes 1540
  1.2 32.3 %copy-start.5 = (bf16[768,384]{1,0:T(8,128)(2,1)S(1)}, bf16[768,384]{1,0:T(8,128)(2,1)}, u32[]{:S(2)}) copy-start(bf16[768,384]{1,0:T(8,128)(2,1)} %refs_4_.1) | copy-start | bytes 1769476
  1.2 13.0 %collective-permute-start.1 = (bf16[1160,128]{1,0:T(8,128)(2,1)S(1)}, bf16[1160,128]{1,0:T(8,128)(2,1)S(1)}, u32[]{:S(2)}, u32[]{:S(2)}) collective-permute-start(bf16[1160,128]{1,0:T(8,128)(2,1)S(1)} %shard_map.74), channel_id=1, source_target_pairs={{0,4},{4,8},{8,12},{12,0},{1,5},{5,9},{9,13},{13,1},{2,6},{6,10},{... | collective-permute-start | bytes 890888 | tf_op jit(solution)/shard_map/ppermute | solution.py:25
  5.3 15.2 %collective-permute-start.4 = (bf16[1152,128]{1,0:T(8,128)(2,1)S(1)}, bf16[1152,128]{1,0:T(8,128)(2,1)S(1)}, u32[]{:S(2)}, u32[]{:S(2)}) collective-permute-start(bf16[1152,128]{1,0:T(8,128)(2,1)S(1)} %shard_map.75), channel_id=1, source_target_pairs={{0,4},{4,8},{8,12},{12,0},{1,5},{5,9},{9,13},{13,1},{2,6},{6,10},{... | collective-permute-start | bytes 884744 | tf_op jit(solution)/shard_map/ppermute | solution.py:25
  14.2 12.7 %collective-permute-start.2 = (bf16[1160,128]{1,0:T(8,128)(2,1)S(1)}, bf16[1160,128]{1,0:T(8,128)(2,1)S(1)}, u32[]{:S(2)}, u32[]{:S(2)}) collective-permute-start(bf16[1160,128]{1,0:T(8,128)(2,1)S(1)} %collective-permute-done.1.piece.marks.refs_0_), channel_id=1, source_target_pairs={{0,4},{4,8},{8,12},{12,0},{1,5},{5,9},{9,13},{13,1},{2,6},{6,10},{... | collective-permute-start | bytes 890888 | tf_op jit(solution)/shard_map/ppermute | solution.py:25
  20.5 12.7 %collective-permute-start.5 = (bf16[1152,128]{1,0:T(8,128)(2,1)S(1)}, bf16[1152,128]{1,0:T(8,128)(2,1)S(1)}, u32[]{:S(2)}, u32[]{:S(2)}) collective-permute-start(bf16[1152,128]{1,0:T(8,128)(2,1)S(1)} %collective-permute-done.4.piece.refs_0_), channel_id=1, source_target_pairs={{0,4},{4,8},{8,12},{12,0},{1,5},{5,9},{9,13},{13,1},{2,6},{6,10},{... | collective-permute-start | bytes 884744 | tf_op jit(solution)/shard_map/ppermute | solution.py:25
  20.5 15.8 %collective-permute-start.21 = (bf16[1152,128]{1,0:T(8,128)(2,1)S(1)}, bf16[1152,128]{1,0:T(8,128)(2,1)S(1)}, u32[]{:S(2)}, u32[]{:S(2)}) collective-permute-start(bf16[1152,128]{1,0:T(8,128)(2,1)S(1)} %collective-permute-done.4.piece.refs_0_), channel_id=1, source_target_pairs={{0,1},{1,0},{2,3},{3,2},{4,5},{5,4},{6,7},{7,6},{8,9},{9,8},{10,11... | collective-permute-start | bytes 884744 | tf_op jit(solution)/shard_map/ppermute | solution.py:25
  20.6 17.6 %collective-permute-start.19 = (bf16[1160,128]{1,0:T(8,128)(2,1)S(1)}, bf16[1160,128]{1,0:T(8,128)(2,1)S(1)}, u32[]{:S(2)}, u32[]{:S(2)}) collective-permute-start(bf16[1160,128]{1,0:T(8,128)(2,1)S(1)} %collective-permute-done.1.piece.marks.refs_0_), channel_id=1, source_target_pairs={{0,1},{1,0},{2,3},{3,2},{4,5},{5,4},{6,7},{7,6},{8,9},{9,8},{10,11... | collective-permute-start | bytes 890888 | tf_op jit(solution)/shard_map/ppermute | solution.py:25
  26.9 12.7 %collective-permute-start.3 = (bf16[1160,128]{1,0:T(8,128)(2,1)S(1)}, bf16[1160,128]{1,0:T(8,128)(2,1)S(1)}, u32[]{:S(2)}, u32[]{:S(2)}) collective-permute-start(bf16[1160,128]{1,0:T(8,128)(2,1)S(1)} %collective-permute-done.2.piece.marks.refs_0_), channel_id=1, source_target_pairs={{0,4},{4,8},{8,12},{12,0},{1,5},{5,9},{9,13},{13,1},{2,6},{6,10},{... | collective-permute-start | bytes 890888 | tf_op jit(solution)/shard_map/ppermute | solution.py:25
  26.9 6.4 %collective-permute-start = (s32[6]{0:T(128)S(1)}, s32[6]{0:T(128)S(1)}, u32[]{:S(2)}, u32[]{:S(2)}) collective-permute-start(s32[6]{0:T(128)S(1)} %copy-done.6), channel_id=1, source_target_pairs={{0,2},{2,0},{1,3},{3,1},{4,6},{6,4},{5,7},{7,5},{8,10},{10,8},{9,1... | collective-permute-start | bytes 80 | tf_op jit(solution)/shard_map/ppermute | solution.py:25
  33.3 8.6 %collective-permute-start.9 = (bf16[576,128]{1,0:T(8,128)(2,1)S(1)}, bf16[576,128]{1,0:T(8,128)(2,1)S(1)}, u32[]{:S(2)}, u32[]{:S(2)}) collective-permute-start(bf16[576,128]{1,0:T(8,128)(2,1)S(1)} %get-tuple-element.20), channel_id=1, source_target_pairs={{0,4},{4,8},{8,12},{12,0},{1,5},{5,9},{9,13},{13,1},{2,6},{6,10},{... | collective-permute-start | bytes 442376 | tf_op jit(solution)/shard_map/ppermute | solution.py:25
  33.3 17.0 %collective-permute-start.14 = (bf16[1152,128]{1,0:T(8,128)(2,1)S(1)}, bf16[1152,128]{1,0:T(8,128)(2,1)S(1)}, u32[]{:S(2)}, u32[]{:S(2)}) collective-permute-start(bf16[1152,128]{1,0:T(8,128)(2,1)S(1)} %collective-permute-done.5.packed.piece.refs_0_), channel_id=1, source_target_pairs={{0,1},{1,0},{2,3},{3,2},{4,5},{5,4},{6,7},{7,6},{8,9},{9,8},{10,11... | collective-permute-start | bytes 884744 | tf_op jit(solution)/shard_map/ppermute | solution.py:25
  36.4 18.6 %collective-permute-start.18 = (f32[3,128,256]{2,1,0:T(8,128)S(1)}, f32[3,128,256]{2,1,0:T(8,128)S(1)}, u32[]{:S(2)}, u32[]{:S(2)}) collective-permute-start(f32[3,128,256]{2,1,0:T(8,128)S(1)} %get-tuple-element.21.refs_0_), channel_id=1, source_target_pairs={{0,2},{2,0},{1,3},{3,1},{4,6},{6,4},{5,7},{7,5},{8,10},{10,8},{9,1... | collective-permute-start | bytes 1179656 | tf_op jit(solution)/shard_map/ppermute | solution.py:25
  38.2 12.7 %collective-permute-start.12 = (bf16[1160,128]{1,0:T(8,128)(2,1)S(1)}, bf16[1160,128]{1,0:T(8,128)(2,1)S(1)}, u32[]{:S(2)}, u32[]{:S(2)}) collective-permute-start(bf16[1160,128]{1,0:T(8,128)(2,1)S(1)} %collective-permute-done.2.piece.marks.refs_0_), channel_id=1, source_target_pairs={{0,1},{1,0},{2,3},{3,2},{4,5},{5,4},{6,7},{7,6},{8,9},{9,8},{10,11... | collective-permute-start | bytes 890888 | tf_op jit(solution)/shard_map/ppermute | solution.py:25
  39.6 11.9 %collective-permute-start.16 = (bf16[1160,128]{1,0:T(8,128)(2,1)S(1)}, bf16[1160,128]{1,0:T(8,128)(2,1)S(1)}, u32[]{:S(2)}, u32[]{:S(2)}) collective-permute-start(bf16[1160,128]{1,0:T(8,128)(2,1)S(1)} %collective-permute-done.3.marks.piece.refs_0_), channel_id=1, source_target_pairs={{0,1},{1,0},{2,3},{3,2},{4,5},{5,4},{6,7},{7,6},{8,9},{9,8},{10,11... | collective-permute-start | bytes 890888 | tf_op jit(solution)/shard_map/ppermute | solution.py:25
  41.9 6.9 %collective-permute-start.6 = (bf16[576,128]{1,0:T(8,128)(2,1)S(1)}, bf16[576,128]{1,0:T(8,128)(2,1)S(1)}, u32[]{:S(2)}, u32[]{:S(2)}) collective-permute-start(bf16[576,128]{1,0:T(8,128)(2,1)S(1)} %get-tuple-element.19), channel_id=1, source_target_pairs={{0,4},{4,8},{8,12},{12,0},{1,5},{5,9},{9,13},{13,1},{2,6},{6,10},{... | collective-permute-start | bytes 442376 | tf_op jit(solution)/shard_map/ppermute | solution.py:25
  48.8 7.7 %collective-permute-start.22 = (f32[3,64,256]{2,1,0:T(8,128)S(1)}, f32[3,64,256]{2,1,0:T(8,128)S(1)}, u32[]{:S(2)}, u32[]{:S(2)}) collective-permute-start(f32[3,64,256]{2,1,0:T(8,128)S(1)} %shard_map.95.refs_6_), channel_id=1, source_target_pairs={{0,2},{2,0},{1,3},{3,1},{4,6},{6,4},{5,7},{7,5},{8,10},{10,8},{9,1... | collective-permute-start | bytes 589832 | tf_op jit(solution)/shard_map/ppermute | solution.py:25
  50.3 8.0 %collective-permute-start.20 = (f32[3,64,256]{2,1,0:T(8,128)S(1)}, f32[3,64,256]{2,1,0:T(8,128)S(1)}, u32[]{:S(2)}, u32[]{:S(2)}) collective-permute-start(f32[3,64,256]{2,1,0:T(8,128)S(1)} %shard_map.92.refs_3_), channel_id=1, source_target_pairs={{0,2},{2,0},{1,3},{3,1},{4,6},{6,4},{5,7},{7,5},{8,10},{10,8},{9,1... | collective-permute-start | bytes 589832 | tf_op jit(solution)/shard_map/ppermute | solution.py:25
  50.9 11.0 %collective-permute-start.10 = (bf16[576,128]{1,0:T(8,128)(2,1)S(1)}, bf16[576,128]{1,0:T(8,128)(2,1)S(1)}, u32[]{:S(2)}, u32[]{:S(2)}) collective-permute-start(bf16[576,128]{1,0:T(8,128)(2,1)S(1)} %collective-permute-done.9.piece.refs_2_), channel_id=1, source_target_pairs={{0,1},{1,0},{2,3},{3,2},{4,5},{5,4},{6,7},{7,6},{8,9},{9,8},{10,11... | collective-permute-start | bytes 442376 | tf_op jit(solution)/shard_map/ppermute | solution.py:25
  51.5 12.0 %collective-permute-start.7 = (bf16[576,128]{1,0:T(8,128)(2,1)S(1)}, bf16[576,128]{1,0:T(8,128)(2,1)S(1)}, u32[]{:S(2)}, u32[]{:S(2)}) collective-permute-start(bf16[576,128]{1,0:T(8,128)(2,1)S(1)} %collective-permute-done.6.piece.refs_0_), channel_id=1, source_target_pairs={{0,1},{1,0},{2,3},{3,2},{4,5},{5,4},{6,7},{7,6},{8,9},{9,8},{10,11... | collective-permute-start | bytes 442376 | tf_op jit(solution)/shard_map/ppermute | solution.py:25
  55.0 12.0 %collective-permute-start.15 = (f32[3,64,256]{2,1,0:T(8,128)S(1)}, f32[3,64,256]{2,1,0:T(8,128)S(1)}, u32[]{:S(2)}, u32[]{:S(2)}) collective-permute-start(f32[3,64,256]{2,1,0:T(8,128)S(1)} %shard_map.86.refs_3_), channel_id=1, source_target_pairs={{0,2},{2,0},{1,3},{3,1},{4,6},{6,4},{5,7},{7,5},{8,10},{10,8},{9,1... | collective-permute-start | bytes 589832 | tf_op jit(solution)/shard_map/ppermute | solution.py:25
  56.5 10.5 %collective-permute-start.13 = (f32[3,64,256]{2,1,0:T(8,128)S(1)}, f32[3,64,256]{2,1,0:T(8,128)S(1)}, u32[]{:S(2)}, u32[]{:S(2)}) collective-permute-start(f32[3,64,256]{2,1,0:T(8,128)S(1)} %shard_map.83.refs_0_), channel_id=1, source_target_pairs={{0,2},{2,0},{1,3},{3,1},{4,6},{6,4},{5,7},{7,5},{8,10},{10,8},{9,1... | collective-permute-start | bytes 589832 | tf_op jit(solution)/shard_map/ppermute | solution.py:25
  58.3 12.9 %collective-permute-start.17 = (f32[3,64,256]{2,1,0:T(8,128)S(1)}, f32[3,64,256]{2,1,0:T(8,128)S(1)}, u32[]{:S(2)}, u32[]{:S(2)}) collective-permute-start(f32[3,64,256]{2,1,0:T(8,128)S(1)} %shard_map.89.refs_6_), channel_id=1, source_target_pairs={{0,2},{2,0},{1,3},{3,1},{4,6},{6,4},{5,7},{7,5},{8,10},{10,8},{9,1... | collective-permute-start | bytes 589832 | tf_op jit(solution)/shard_map/ppermute | solution.py:25
  62.4 10.9 %collective-permute-start.11 = (f32[3,32,256]{2,1,0:T(8,128)S(1)}, f32[3,32,256]{2,1,0:T(8,128)S(1)}, u32[]{:S(2)}, u32[]{:S(2)}) collective-permute-start(f32[3,32,256]{2,1,0:T(8,128)S(1)} %shard_map.80.refs_2_), channel_id=1, source_target_pairs={{0,2},{2,0},{1,3},{3,1},{4,6},{6,4},{5,7},{7,5},{8,10},{10,8},{9,1... | collective-permute-start | bytes 294920 | tf_op jit(solution)/shard_map/ppermute | solution.py:25
  63.9 10.9 %collective-permute-start.8 = (f32[3,32,256]{2,1,0:T(8,128)S(1)}, f32[3,32,256]{2,1,0:T(8,128)S(1)}, u32[]{:S(2)}, u32[]{:S(2)}) collective-permute-start(f32[3,32,256]{2,1,0:T(8,128)S(1)} %shard_map.78.refs_0_), channel_id=1, source_target_pairs={{0,2},{2,0},{1,3},{3,1},{4,6},{6,4},{5,7},{7,5},{8,10},{10,8},{9,1... | collective-permute-start | bytes 294920 | tf_op jit(solution)/shard_map/ppermute | solution.py:25
  71.2 3.6 %copy-start.3 = (bf16[384,768]{1,0:T(8,128)(2,1)S(1)}, bf16[384,768]{1,0:T(8,128)(2,1)}, u32[]{:S(2)}) copy-start(bf16[384,768]{1,0:T(8,128)(2,1)} %w_out.1) | copy-start | bytes 1769476
  75.7 2.1 %collective-permute-start.23 = (bf16[6,128,384]{2,1,0:T(8,128)(2,1)S(1)}, bf16[6,128,384]{2,1,0:T(8,128)(2,1)S(1)}, u32[]{:S(2)}, u32[]{:S(2)}) collective-permute-start(bf16[6,128,384]{2,1,0:T(8,128)(2,1)S(1)} %get-tuple-element.30), channel_id=1, source_target_pairs={{0,1},{1,0},{2,3},{3,2},{4,5},{5,4},{6,7},{7,6},{8,9},{9,8},{10,11... | collective-permute-start | bytes 1769480 | tf_op jit(solution)/shard_map/ppermute | solution.py:25
where the time goes:
time: 78.9 us; the launch traced here: 78.7 us
  waiting for transfers between devices  42.1 us (53%)
  Pallas kernels  18.2 us (23%)
  starting transfers between devices  17.1 us (22%)
  other arithmetic  0.97 us (1%)
    ppermute x24, waiting for transfers between devices, ring(): lax.ppermute(value, axis, [(i, (i + by) % length) for i in range(length)])  42.1 us
    ppermute x24, starting transfers between devices, ring(): lax.ppermute(value, axis, [(i, (i + by) % length) for i in range(length)])  17.1 us
    pallas_call x26, Pallas kernels, call(): pl.pallas_call(kernel, out_shape=out_shape, in_specs=specs, out_specs=who...  16 us
    pallas_call x2, Pallas kernels, shards(): pl.pallas_call(functools.partial(pack_kernel, chunk=k, share=share), out_...  2.16 us
  transfers between devices with their start and end apart: 24, of which 12 were waited for; matrix products, arithmetic and copies ran while one was open for 0% of the time, Pallas kernels for 21%

commit v1 on v0

--- a/solution.py
+++ b/solution.py
@@ -14,6 +14,7 @@
 PER_TILE = LANES // HEAD_DIM
 CHUNKS = 2
 MARK_ROWS = 8
+CLOSED = 0
 PIECE = 32
 PARTS = HEAD_DIM // PIECE
 MASKED = -1000000000.0
@@ -23,6 +24,14 @@
 def ring(value, axis, by=1):
     length = lax.axis_size(axis)
     return lax.ppermute(value, axis, [(i, (i + by) % length) for i in range(length)])
+
+
+def pass_on(value):
+    length = lax.axis_size("res")
+    stops = list(range(length))
+    if math.prod(lax.axis_size(axis) for axis in ("grp", "res", "seq", "head")) < CLOSED:
+        stops = stops[::2] + stops[1::2][::-1]
+    return lax.ppermute(value, "res", [(stops[i - 1], stops[i]) for i in range(length)])
 
 
 def whole(count):
@@ -397,9 +406,9 @@
                 [moving[tail]],
                 0,
             )
-            fine = [ring(fine[n], "res") for n in range(PARTS)]
+            fine = [pass_on(fine[n]) for n in range(PARTS)]
         count = tail if step == last else CHUNKS
-        moving = [ring(moving[k], "res") for k in range(count)]
+        moving = [pass_on(moving[k]) for k in range(count)]
         moved[step] = moving[0]
         for k in range(count):
             pieces[step, k] = shared_rows(moving[k])

time: 78.9 us -> 78.9 us (level)
    ppermute x0 -> x7, waiting for transfers between devices: none -> 32.2 us  [pass_on(): lax.ppermute(value, 'res', [(stops[i - 1], stops[i]) for i in range(lengt...]
    ppermute x24 -> x17, waiting for transfers between devices: 42.1 us -> 9.89 us  [ring(): lax.ppermute(value, axis, [(i, (i + by) % length) for i in range(length)])]
    ppermute x0 -> x7, starting transfers between devices: none -> 4.8 us  [pass_on(): lax.ppermute(value, 'res', [(stops[i - 1], stops[i]) for i in range(lengt...]
    ppermute x24 -> x17, starting transfers between devices: 17.1 us -> 12.3 us  [ring(): lax.ppermute(value, axis, [(i, (i + by) % length) for i in range(length)])]
where the time goes in v1:
time: 78.9 us; the launch traced here: 78.7 us
  waiting for transfers between devices  42.1 us (53%)
  Pallas kernels  18.2 us (23%)
  starting transfers between devices  17.1 us (22%)
  other arithmetic  0.97 us (1%)
    ppermute x7, waiting for transfers between devices, pass_on(): lax.ppermute(value, 'res', [(stops[i - 1], stops[i]) for i in range(lengt...  32.2 us
    pallas_call x26, Pallas kernels, call(): pl.pallas_call(kernel, out_shape=out_shape, in_specs=specs, out_specs=who...  16 us
    ppermute x17, starting transfers between devices, ring(): lax.ppermute(value, axis, [(i, (i + by) % length) for i in range(length)])  12.3 us
    ppermute x17, waiting for transfers between devices, ring(): lax.ppermute(value, axis, [(i, (i + by) % length) for i in range(length)])  9.89 us
    ppermute x7, starting transfers between devices, pass_on(): lax.ppermute(value, 'res', [(stops[i - 1], stops[i]) for i in range(lengt...  4.8 us
    pallas_call x2, Pallas kernels, shards(): pl.pallas_call(functools.partial(pack_kernel, chunk=k, share=share), out_...  2.16 us
  transfers between devices with their start and end apart: 24, of which 12 were waited for; matrix products, arithmetic and copies ran while one was open for 0% of the time, Pallas kernels for 21%

profile of v1, /device:TPU:0, one launch (start us, length us, event | category | flops | bytes accessed | tf_op | source)
XLA Modules:
  0.0 78.7 jit_solution(2551164957627771469)
XLA Ops:
  0.0 1.1 %shard_map.74 = bf16[1160,128]{1,0:T(8,128)(2,1)S(1)} custom-call(bf16[6,128,768]{2,1,0:T(8,128)(2,1)} %tokens.3, s32[1,128]{1,0:T(1,128)} %bitcast.1), custom_call_target="tpu_custom_call" | custom-call | tf_op jit(solution)/shard_map/pallas_call | solution.py:356
  1.1 0.0 copy-start
  1.2 0.0 copy-start.1
  1.2 0.0 copy-start.4
  1.2 0.0 copy-start.5
  1.2 3.1 %collective-permute-start.1 = (bf16[1160,128]{1,0:T(8,128)(2,1)S(1)}, bf16[1160,128]{1,0:T(8,128)(2,1)S(1)}, u32[]{:S(2)}, u32[]{:S(2)}) collective-permute-start(bf16[1160,128]{1,0:T(8,128)(2,1)S(1)} %shard_map.74), channel_id=1, source_target_pairs={{12,0},{0,4},{4,8},{8,12},{13,1},{1,5},{5,9},{9,13},{14,2},{2,6},{... | collective-permute-start | bytes 890888 | tf_op jit(solution)/shard_map/ppermute | solution.py:34
  4.3 1.0 %shard_map.75 = bf16[1152,128]{1,0:T(8,128)(2,1)S(1)} custom-call(bf16[6,128,768]{2,1,0:T(8,128)(2,1)} %tokens.3, s32[1,128]{1,0:T(1,128)} %bitcast.2), custom_call_target="tpu_custom_call" | custom-call | tf_op jit(solution)/shard_map/pallas_call | solution.py:356
  5.3 1.6 %collective-permute-start.4 = (bf16[1152,128]{1,0:T(8,128)(2,1)S(1)}, bf16[1152,128]{1,0:T(8,128)(2,1)S(1)}, u32[]{:S(2)}, u32[]{:S(2)}) collective-permute-start(bf16[1152,128]{1,0:T(8,128)(2,1)S(1)} %shard_map.75), channel_id=1, source_target_pairs={{12,0},{0,4},{4,8},{8,12},{13,1},{1,5},{5,9},{9,13},{14,2},{2,6},{... | collective-permute-start | bytes 884744 | tf_op jit(solution)/shard_map/ppermute | solution.py:34
  7.0 7.3 %collective-permute-done.1.piece.marks.refs_0_ = bf16[1160,128]{1,0:T(8,128)(2,1)S(1)} collective-permute-done((bf16[1160,128]{1,0:T(8,128)(2,1)S(1)}, bf16[1160,128]{1,0:T(8,128)(2,1)S(1)}, u32[]{:S(2)}, u32[]{:S(2)}) %collective-permute-start.1) | collective-permute-done | bytes 296992 | tf_op jit(solution)/shard_map/ppermute | solution.py:34
  14.2 6.3 %collective-permute-done.4.piece.refs_0_ = bf16[1152,128]{1,0:T(8,128)(2,1)S(1)} collective-permute-done((bf16[1152,128]{1,0:T(8,128)(2,1)S(1)}, bf16[1152,128]{1,0:T(8,128)(2,1)S(1)}, u32[]{:S(2)}, u32[]{:S(2)}) %collective-permute-start.4) | collective-permute-done | bytes 294944 | tf_op jit(solution)/shard_map/ppermute | solution.py:34
  20.5 0.0 collective-permute-start.21
  20.6 0.5 collective-permute-start.19
  21.1 5.8 %collective-permute-done.2.piece.marks.refs_0_ = bf16[1160,128]{1,0:T(8,128)(2,1)S(1)} collective-permute-done((bf16[1160,128]{1,0:T(8,128)(2,1)S(1)}, bf16[1160,128]{1,0:T(8,128)(2,1)S(1)}, u32[]{:S(2)}, u32[]{:S(2)}) %collective-permute-start.2) | collective-permute-done | bytes 296992 | tf_op jit(solution)/shard_map/ppermute | solution.py:34
  26.9 1.7 %collective-permute-start = (s32[6]{0:T(128)S(1)}, s32[6]{0:T(128)S(1)}, u32[]{:S(2)}, u32[]{:S(2)}) collective-permute-start(s32[6]{0:T(128)S(1)} %copy-done.6), channel_id=1, source_target_pairs={{0,2},{2,0},{1,3},{3,1},{4,6},{6,4},{5,7},{7,5},{8,10},{10,8},{9,1... | collective-permute-start | bytes 80 | tf_op jit(solution)/shard_map/ppermute | solution.py:26
  28.6 4.6 %collective-permute-done.5.packed.piece.refs_0_ = bf16[1152,128]{1,0:T(8,128)(2,1)S(1)} collective-permute-done((bf16[1152,128]{1,0:T(8,128)(2,1)S(1)}, bf16[1152,128]{1,0:T(8,128)(2,1)S(1)}, u32[]{:S(2)}, u32[]{:S(2)}) %collective-permute-start.5) | collective-permute-done | bytes 294944 | tf_op jit(solution)/shard_map/ppermute | solution.py:34
  33.3 0.1 collective-permute-start.9
  33.3 0.1 collective-permute-start.14
  33.5 2.9 %shard_map.73 = (bf16[3,256,768]{2,1,0:T(8,128)(2,1)S(1)}, f32[3,128,256]{2,1,0:T(8,128)S(1)}, bf16[2,3,128,768]{3,2,1,0:T(8,128)(2,1)S(1)}) custom-call(s32[6]{0:T(128)S(1)} %copy-done.6, s32[6]{0:T(128)S(1)} %collective-permute-done.refs_1_, s32[1,128]{1,0:T(1,128)S(1)} %bitcast.3, bf16[6,128,768]{2,1,0:T(8,128)(2,1)S(1)} %copy-done.2, ...), custom_call_target="tpu_custom_call" | custom-call | flops 1509949440 | bytes 2949680 | tf_op jit(solution)/shard_map/pallas_call | solution.py:45
  36.4 1.8 %collective-permute-start.18 = (f32[3,128,256]{2,1,0:T(8,128)S(1)}, f32[3,128,256]{2,1,0:T(8,128)S(1)}, u32[]{:S(2)}, u32[]{:S(2)}) collective-permute-start(f32[3,128,256]{2,1,0:T(8,128)S(1)} %get-tuple-element.21.refs_0_), channel_id=1, source_target_pairs={{0,2},{2,0},{1,3},{3,1},{4,6},{6,4},{5,7},{7,5},{8,10},{10,8},{9,1... | collective-permute-start | bytes 1179656 | tf_op jit(solution)/shard_map/ppermute | solution.py:26
  38.2 0.2 collective-permute-start.12
  38.4 1.2 %collective-permute-done.3.marks.piece.refs_0_ = bf16[1160,128]{1,0:T(8,128)(2,1)S(1)} collective-permute-done((bf16[1160,128]{1,0:T(8,128)(2,1)S(1)}, bf16[1160,128]{1,0:T(8,128)(2,1)S(1)}, u32[]{:S(2)}, u32[]{:S(2)}) %collective-permute-start.3) | collective-permute-done | bytes 296992 | tf_op jit(solution)/shard_map/ppermute | solution.py:34
  39.6 2.3 %collective-permute-done.9.piece.refs_2_ = bf16[576,128]{1,0:T(8,128)(2,1)S(1)} collective-permute-done((bf16[576,128]{1,0:T(8,128)(2,1)S(1)}, bf16[576,128]{1,0:T(8,128)(2,1)S(1)}, u32[]{:S(2)}, u32[]{:S(2)}) %collective-permute-start.9) | collective-permute-done | bytes 147488 | tf_op jit(solution)/shard_map/ppermute | solution.py:34
  41.9 0.0 collective-permute-start.6
  41.9 0.6 shard_map.94.before
  42.5 0.6 shard_map.91.before
  43.1 0.6 shard_map.95.refs_6_
  43.7 0.6 shard_map.92.refs_3_
  44.2 4.6 %collective-permute-done.6.piece.refs_0_ = bf16[576,128]{1,0:T(8,128)(2,1)S(1)} collective-permute-done((bf16[576,128]{1,0:T(8,128)(2,1)S(1)}, bf16[576,128]{1,0:T(8,128)(2,1)S(1)}, u32[]{:S(2)}, u32[]{:S(2)}) %collective-permute-start.6) | collective-permute-done | bytes 147488 | tf_op jit(solution)/shard_map/ppermute | solution.py:34
  48.8 1.5 %collective-permute-start.22 = (f32[3,64,256]{2,1,0:T(8,128)S(1)}, f32[3,64,256]{2,1,0:T(8,128)S(1)}, u32[]{:S(2)}, u32[]{:S(2)}) collective-permute-start(f32[3,64,256]{2,1,0:T(8,128)S(1)} %shard_map.95.refs_6_), channel_id=1, source_target_pairs={{0,2},{2,0},{1,3},{3,1},{4,6},{6,4},{5,7},{7,5},{8,10},{10,8},{9,1... | collective-permute-start | bytes 589832 | tf_op jit(solution)/shard_map/ppermute | solution.py:26
  50.3 0.5 collective-permute-start.20
  50.9 0.6 shard_map.85.before
  51.5 0.6 collective-permute-start.7
  52.0 0.6 shard_map.82.before
  52.6 0.6 shard_map.86.refs_3_
  53.2 0.6 shard_map.88.before
  53.8 0.6 shard_map.83.refs_0_
  54.4 0.6 shard_map.89.refs_6_
  55.0 1.6 %collective-permute-start.15 = (f32[3,64,256]{2,1,0:T(8,128)S(1)}, f32[3,64,256]{2,1,0:T(8,128)S(1)}, u32[]{:S(2)}, u32[]{:S(2)}) collective-permute-start(f32[3,64,256]{2,1,0:T(8,128)S(1)} %shard_map.86.refs_3_), channel_id=1, source_target_pairs={{0,2},{2,0},{1,3},{3,1},{4,6},{6,4},{5,7},{7,5},{8,10},{10,8},{9,1... | collective-permute-start | bytes 589832 | tf_op jit(solution)/shard_map/ppermute | solution.py:26
  56.5 0.6 collective-permute-start.13
  57.1 1.2 %collective-permute-done.20.refs_4_ = f32[3,64,256]{2,1,0:T(8,128)S(1)} collective-permute-done((f32[3,64,256]{2,1,0:T(8,128)S(1)}, f32[3,64,256]{2,1,0:T(8,128)S(1)}, u32[]{:S(2)}, u32[]{:S(2)}) %collective-permute-start.20) | collective-permute-done | bytes 196640 | tf_op jit(solution)/shard_map/ppermute | solution.py:26
  58.3 1.1 %collective-permute-start.17 = (f32[3,64,256]{2,1,0:T(8,128)S(1)}, f32[3,64,256]{2,1,0:T(8,128)S(1)}, u32[]{:S(2)}, u32[]{:S(2)}) collective-permute-start(f32[3,64,256]{2,1,0:T(8,128)S(1)} %shard_map.89.refs_6_), channel_id=1, source_target_pairs={{0,2},{2,0},{1,3},{3,1},{4,6},{6,4},{5,7},{7,5},{8,10},{10,8},{9,1... | collective-permute-start | bytes 589832 | tf_op jit(solution)/shard_map/ppermute | solution.py:26
  59.4 0.5 shard_map.96.refs_8_
  59.8 0.5 shard_map.93.refs_5_
  60.3 0.5 shard_map.79.before
  60.8 0.5 shard_map.77.before
  61.3 0.6 shard_map.97
  61.9 0.5 shard_map.80.refs_2_
  62.4 1.0 %collective-permute-start.11 = (f32[3,32,256]{2,1,0:T(8,128)S(1)}, f32[3,32,256]{2,1,0:T(8,128)S(1)}, u32[]{:S(2)}, u32[]{:S(2)}) collective-permute-start(f32[3,32,256]{2,1,0:T(8,128)S(1)} %shard_map.80.refs_2_), channel_id=1, source_target_pairs={{0,2},{2,0},{1,3},{3,1},{4,6},{6,4},{5,7},{7,5},{8,10},{10,8},{9,1... | collective-permute-start | bytes 294920 | tf_op jit(solution)/shard_map/ppermute | solution.py:26
  63.4 0.5 shard_map.78.refs_0_
  63.9 1.1 %collective-permute-start.8 = (f32[3,32,256]{2,1,0:T(8,128)S(1)}, f32[3,32,256]{2,1,0:T(8,128)S(1)}, u32[]{:S(2)}, u32[]{:S(2)}) collective-permute-start(f32[3,32,256]{2,1,0:T(8,128)S(1)} %shard_map.78.refs_0_), channel_id=1, source_target_pairs={{0,2},{2,0},{1,3},{3,1},{4,6},{6,4},{5,7},{7,5},{8,10},{10,8},{9,1... | collective-permute-start | bytes 294920 | tf_op jit(solution)/shard_map/ppermute | solution.py:26
  65.0 0.5 shard_map.87.refs_5_
  65.5 0.5 shard_map.81.refs_4_
  66.0 0.5 shard_map.84.refs_2_
  66.5 0.5 shard_map.90.refs_8_
  67.0 0.0 collective-permute-done.13.refs_1_
  67.0 4.2 %collective-permute-done.17.refs_7_ = f32[3,64,256]{2,1,0:T(8,128)S(1)} collective-permute-done((f32[3,64,256]{2,1,0:T(8,128)S(1)}, f32[3,64,256]{2,1,0:T(8,128)S(1)}, u32[]{:S(2)}, u32[]{:S(2)}) %collective-permute-start.17) | collective-permute-done | bytes 196640 | tf_op jit(solution)/shard_map/ppermute | solution.py:26
  71.2 0.6 shard_map.98
  71.8 1.5 %collective-permute-done.11.refs_3_ = f32[3,32,256]{2,1,0:T(8,128)S(1)} collective-permute-done((f32[3,32,256]{2,1,0:T(8,128)S(1)}, f32[3,32,256]{2,1,0:T(8,128)S(1)}, u32[]{:S(2)}, u32[]{:S(2)}) %collective-permute-start.11) | collective-permute-done | bytes 98336 | tf_op jit(solution)/shard_map/ppermute | solution.py:26
  73.3 1.5 %collective-permute-done.8.refs_1_ = f32[3,32,256]{2,1,0:T(8,128)S(1)} collective-permute-done((f32[3,32,256]{2,1,0:T(8,128)S(1)}, f32[3,32,256]{2,1,0:T(8,128)S(1)}, u32[]{:S(2)}, u32[]{:S(2)}) %collective-permute-start.8) | collective-permute-done | bytes 98336 | tf_op jit(solution)/shard_map/ppermute | solution.py:26
  74.8 0.9 %shard_map.99 = (bf16[6,128,384]{2,1,0:T(8,128)(2,1)S(1)}, bf16[6,128,384]{2,1,0:T(8,128)(2,1)S(1)}) custom-call(f32[3,32,256]{2,1,0:T(8,128)S(1)} %shard_map.78.refs_0_, f32[3,32,256]{2,1,0:T(8,128)S(1)} %collective-permute-done.8.refs_1_, f32[3,32,256]{2,1,0:T(8,128)S(1)} %shard_map.80.refs_2_, f32[3,32,256]{2,1,0:T(8,128)S(1)} %collective-permute-done.11.refs_3_, ...), custom_call_target="tpu_custom_call" | custom-call | flops 301989888 | bytes 2801664 | tf_op jit(solution)/shard_map/pallas_call | solution.py:45
  75.7 0.1 collective-permute-start.23
  75.8 0.5 shard_map.100
  76.3 1.4 %collective-permute-done.23 = bf16[6,128,384]{2,1,0:T(8,128)(2,1)S(1)} collective-permute-done((bf16[6,128,384]{2,1,0:T(8,128)(2,1)S(1)}, bf16[6,128,384]{2,1,0:T(8,128)(2,1)S(1)}, u32[]{:S(2)}, u32[]{:S(2)}) %collective-permute-start.23) | collective-permute-done | bytes 589856 | tf_op jit(solution)/shard_map/ppermute | solution.py:26
  77.8 1.0 %add_convert_fusion = bf16[6,128,384]{2,1,0:T(8,128)(2,1)} fusion(f32[6,128,384]{2,1,0:T(8,128)S(1)} %shard_map.100, bf16[6,128,384]{2,1,0:T(8,128)(2,1)S(1)} %collective-permute-done.23), kind=kLoop, calls=%fused_computation | loop fusion | flops 884736 | bytes 2359296 | tf_op jit(solution)/shard_map/convert_element_type | solution.py:508
  (27 shorter events, 0.1 us)
Async XLA Ops:
  0.0 26.9 %copy-start.6 = (s32[6]{0:T(128)S(1)}, s32[6]{0:T(128)}, u32[]{:S(2)}) copy-start(s32[6]{0:T(128)} %refs_0_.1) | copy-start | bytes 76
  0.0 33.4 %copy-start.2 = (bf16[6,128,768]{2,1,0:T(8,128)(2,1)S(1)}, bf16[6,128,768]{2,1,0:T(8,128)(2,1)}, u32[]{:S(2)}) copy-start(bf16[6,128,768]{2,1,0:T(8,128)(2,1)} %tokens.3) | copy-start | bytes 3538948
  1.1 32.3 %copy-start = (bf16[768,384]{1,0:T(8,128)(2,1)S(1)}, bf16[768,384]{1,0:T(8,128)(2,1)}, u32[]{:S(2)}) copy-start(bf16[768,384]{1,0:T(8,128)(2,1)} %w_key.27) | copy-start | bytes 1769476
  1.2 32.3 %copy-start.1 = (bf16[768,384]{1,0:T(8,128)(2,1)S(1)}, bf16[768,384]{1,0:T(8,128)(2,1)}, u32[]{:S(2)}) copy-start(bf16[768,384]{1,0:T(8,128)(2,1)} %w_value.11) | copy-start | bytes 1769476
  1.2 32.3 %copy-start.4 = (s32[128]{0:T(128)S(1)}, s32[128]{0:T(128)}, u32[]{:S(2)}) copy-start(s32[128]{0:T(128)} %param.9) | copy-start | bytes 1540
  1.2 32.3 %copy-start.5 = (bf16[768,384]{1,0:T(8,128)(2,1)S(1)}, bf16[768,384]{1,0:T(8,128)(2,1)}, u32[]{:S(2)}) copy-start(bf16[768,384]{1,0:T(8,128)(2,1)} %refs_4_.1) | copy-start | bytes 1769476
  1.2 13.0 %collective-permute-start.1 = (bf16[1160,128]{1,0:T(8,128)(2,1)S(1)}, bf16[1160,128]{1,0:T(8,128)(2,1)S(1)}, u32[]{:S(2)}, u32[]{:S(2)}) collective-permute-start(bf16[1160,128]{1,0:T(8,128)(2,1)S(1)} %shard_map.74), channel_id=1, source_target_pairs={{12,0},{0,4},{4,8},{8,12},{13,1},{1,5},{5,9},{9,13},{14,2},{2,6},{... | collective-permute-start | bytes 890888 | tf_op jit(solution)/shard_map/ppermute | solution.py:34
  5.3 15.2 %collective-permute-start.4 = (bf16[1152,128]{1,0:T(8,128)(2,1)S(1)}, bf16[1152,128]{1,0:T(8,128)(2,1)S(1)}, u32[]{:S(2)}, u32[]{:S(2)}) collective-permute-start(bf16[1152,128]{1,0:T(8,128)(2,1)S(1)} %shard_map.75), channel_id=1, source_target_pairs={{12,0},{0,4},{4,8},{8,12},{13,1},{1,5},{5,9},{9,13},{14,2},{2,6},{... | collective-permute-start | bytes 884744 | tf_op jit(solution)/shard_map/ppermute | solution.py:34
  14.2 12.7 %collective-permute-start.2 = (bf16[1160,128]{1,0:T(8,128)(2,1)S(1)}, bf16[1160,128]{1,0:T(8,128)(2,1)S(1)}, u32[]{:S(2)}, u32[]{:S(2)}) collective-permute-start(bf16[1160,128]{1,0:T(8,128)(2,1)S(1)} %collective-permute-done.1.piece.marks.refs_0_), channel_id=1, source_target_pairs={{12,0},{0,4},{4,8},{8,12},{13,1},{1,5},{5,9},{9,13},{14,2},{2,6},{... | collective-permute-start | bytes 890888 | tf_op jit(solution)/shard_map/ppermute | solution.py:34
  20.5 12.7 %collective-permute-start.5 = (bf16[1152,128]{1,0:T(8,128)(2,1)S(1)}, bf16[1152,128]{1,0:T(8,128)(2,1)S(1)}, u32[]{:S(2)}, u32[]{:S(2)}) collective-permute-start(bf16[1152,128]{1,0:T(8,128)(2,1)S(1)} %collective-permute-done.4.piece.refs_0_), channel_id=1, source_target_pairs={{12,0},{0,4},{4,8},{8,12},{13,1},{1,5},{5,9},{9,13},{14,2},{2,6},{... | collective-permute-start | bytes 884744 | tf_op jit(solution)/shard_map/ppermute | solution.py:34
  20.5 15.8 %collective-permute-start.21 = (bf16[1152,128]{1,0:T(8,128)(2,1)S(1)}, bf16[1152,128]{1,0:T(8,128)(2,1)S(1)}, u32[]{:S(2)}, u32[]{:S(2)}) collective-permute-start(bf16[1152,128]{1,0:T(8,128)(2,1)S(1)} %collective-permute-done.4.piece.refs_0_), channel_id=1, source_target_pairs={{0,1},{1,0},{2,3},{3,2},{4,5},{5,4},{6,7},{7,6},{8,9},{9,8},{10,11... | collective-permute-start | bytes 884744 | tf_op jit(solution)/shard_map/ppermute | solution.py:26
  20.6 17.6 %collective-permute-start.19 = (bf16[1160,128]{1,0:T(8,128)(2,1)S(1)}, bf16[1160,128]{1,0:T(8,128)(2,1)S(1)}, u32[]{:S(2)}, u32[]{:S(2)}) collective-permute-start(bf16[1160,128]{1,0:T(8,128)(2,1)S(1)} %collective-permute-done.1.piece.marks.refs_0_), channel_id=1, source_target_pairs={{0,1},{1,0},{2,3},{3,2},{4,5},{5,4},{6,7},{7,6},{8,9},{9,8},{10,11... | collective-permute-start | bytes 890888 | tf_op jit(solution)/shard_map/ppermute | solution.py:26
  26.9 12.7 %collective-permute-start.3 = (bf16[1160,128]{1,0:T(8,128)(2,1)S(1)}, bf16[1160,128]{1,0:T(8,128)(2,1)S(1)}, u32[]{:S(2)}, u32[]{:S(2)}) collective-permute-start(bf16[1160,128]{1,0:T(8,128)(2,1)S(1)} %collective-permute-done.2.piece.marks.refs_0_), channel_id=1, source_target_pairs={{12,0},{0,4},{4,8},{8,12},{13,1},{1,5},{5,9},{9,13},{14,2},{2,6},{... | collective-permute-start | bytes 890888 | tf_op jit(solution)/shard_map/ppermute | solution.py:34
  26.9 6.4 %collective-permute-start = (s32[6]{0:T(128)S(1)}, s32[6]{0:T(128)S(1)}, u32[]{:S(2)}, u32[]{:S(2)}) collective-permute-start(s32[6]{0:T(128)S(1)} %copy-done.6), channel_id=1, source_target_pairs={{0,2},{2,0},{1,3},{3,1},{4,6},{6,4},{5,7},{7,5},{8,10},{10,8},{9,1... | collective-permute-start | bytes 80 | tf_op jit(solution)/shard_map/ppermute | solution.py:26
  33.3 8.6 %collective-permute-start.9 = (bf16[576,128]{1,0:T(8,128)(2,1)S(1)}, bf16[576,128]{1,0:T(8,128)(2,1)S(1)}, u32[]{:S(2)}, u32[]{:S(2)}) collective-permute-start(bf16[576,128]{1,0:T(8,128)(2,1)S(1)} %get-tuple-element.20), channel_id=1, source_target_pairs={{12,0},{0,4},{4,8},{8,12},{13,1},{1,5},{5,9},{9,13},{14,2},{2,6},{... | collective-permute-start | bytes 442376 | tf_op jit(solution)/shard_map/ppermute | solution.py:34
  33.3 17.0 %collective-permute-start.14 = (bf16[1152,128]{1,0:T(8,128)(2,1)S(1)}, bf16[1152,128]{1,0:T(8,128)(2,1)S(1)}, u32[]{:S(2)}, u32[]{:S(2)}) collective-permute-start(bf16[1152,128]{1,0:T(8,128)(2,1)S(1)} %collective-permute-done.5.packed.piece.refs_0_), channel_id=1, source_target_pairs={{0,1},{1,0},{2,3},{3,2},{4,5},{5,4},{6,7},{7,6},{8,9},{9,8},{10,11... | collective-permute-start | bytes 884744 | tf_op jit(solution)/shard_map/ppermute | solution.py:26
  36.4 18.6 %collective-permute-start.18 = (f32[3,128,256]{2,1,0:T(8,128)S(1)}, f32[3,128,256]{2,1,0:T(8,128)S(1)}, u32[]{:S(2)}, u32[]{:S(2)}) collective-permute-start(f32[3,128,256]{2,1,0:T(8,128)S(1)} %get-tuple-element.21.refs_0_), channel_id=1, source_target_pairs={{0,2},{2,0},{1,3},{3,1},{4,6},{6,4},{5,7},{7,5},{8,10},{10,8},{9,1... | collective-permute-start | bytes 1179656 | tf_op jit(solution)/shard_map/ppermute | solution.py:26
  38.2 12.7 %collective-permute-start.12 = (bf16[1160,128]{1,0:T(8,128)(2,1)S(1)}, bf16[1160,128]{1,0:T(8,128)(2,1)S(1)}, u32[]{:S(2)}, u32[]{:S(2)}) collective-permute-start(bf16[1160,128]{1,0:T(8,128)(2,1)S(1)} %collective-permute-done.2.piece.marks.refs_0_), channel_id=1, source_target_pairs={{0,1},{1,0},{2,3},{3,2},{4,5},{5,4},{6,7},{7,6},{8,9},{9,8},{10,11... | collective-permute-start | bytes 890888 | tf_op jit(solution)/shard_map/ppermute | solution.py:26
  39.6 11.9 %collective-permute-start.16 = (bf16[1160,128]{1,0:T(8,128)(2,1)S(1)}, bf16[1160,128]{1,0:T(8,128)(2,1)S(1)}, u32[]{:S(2)}, u32[]{:S(2)}) collective-permute-start(bf16[1160,128]{1,0:T(8,128)(2,1)S(1)} %collective-permute-done.3.marks.piece.refs_0_), channel_id=1, source_target_pairs={{0,1},{1,0},{2,3},{3,2},{4,5},{5,4},{6,7},{7,6},{8,9},{9,8},{10,11... | collective-permute-start | bytes 890888 | tf_op jit(solution)/shard_map/ppermute | solution.py:26
  41.9 6.9 %collective-permute-start.6 = (bf16[576,128]{1,0:T(8,128)(2,1)S(1)}, bf16[576,128]{1,0:T(8,128)(2,1)S(1)}, u32[]{:S(2)}, u32[]{:S(2)}) collective-permute-start(bf16[576,128]{1,0:T(8,128)(2,1)S(1)} %get-tuple-element.19), channel_id=1, source_target_pairs={{12,0},{0,4},{4,8},{8,12},{13,1},{1,5},{5,9},{9,13},{14,2},{2,6},{... | collective-permute-start | bytes 442376 | tf_op jit(solution)/shard_map/ppermute | solution.py:34
  48.8 7.7 %collective-permute-start.22 = (f32[3,64,256]{2,1,0:T(8,128)S(1)}, f32[3,64,256]{2,1,0:T(8,128)S(1)}, u32[]{:S(2)}, u32[]{:S(2)}) collective-permute-start(f32[3,64,256]{2,1,0:T(8,128)S(1)} %shard_map.95.refs_6_), channel_id=1, source_target_pairs={{0,2},{2,0},{1,3},{3,1},{4,6},{6,4},{5,7},{7,5},{8,10},{10,8},{9,1... | collective-permute-start | bytes 589832 | tf_op jit(solution)/shard_map/ppermute | solution.py:26
  50.3 8.0 %collective-permute-start.20 = (f32[3,64,256]{2,1,0:T(8,128)S(1)}, f32[3,64,256]{2,1,0:T(8,128)S(1)}, u32[]{:S(2)}, u32[]{:S(2)}) collective-permute-start(f32[3,64,256]{2,1,0:T(8,128)S(1)} %shard_map.92.refs_3_), channel_id=1, source_target_pairs={{0,2},{2,0},{1,3},{3,1},{4,6},{6,4},{5,7},{7,5},{8,10},{10,8},{9,1... | collective-permute-start | bytes 589832 | tf_op jit(solution)/shard_map/ppermute | solution.py:26
  50.9 11.0 %collective-permute-start.10 = (bf16[576,128]{1,0:T(8,128)(2,1)S(1)}, bf16[576,128]{1,0:T(8,128)(2,1)S(1)}, u32[]{:S(2)}, u32[]{:S(2)}) collective-permute-start(bf16[576,128]{1,0:T(8,128)(2,1)S(1)} %collective-permute-done.9.piece.refs_2_), channel_id=1, source_target_pairs={{0,1},{1,0},{2,3},{3,2},{4,5},{5,4},{6,7},{7,6},{8,9},{9,8},{10,11... | collective-permute-start | bytes 442376 | tf_op jit(solution)/shard_map/ppermute | solution.py:26
  51.5 12.0 %collective-permute-start.7 = (bf16[576,128]{1,0:T(8,128)(2,1)S(1)}, bf16[576,128]{1,0:T(8,128)(2,1)S(1)}, u32[]{:S(2)}, u32[]{:S(2)}) collective-permute-start(bf16[576,128]{1,0:T(8,128)(2,1)S(1)} %collective-permute-done.6.piece.refs_0_), channel_id=1, source_target_pairs={{0,1},{1,0},{2,3},{3,2},{4,5},{5,4},{6,7},{7,6},{8,9},{9,8},{10,11... | collective-permute-start | bytes 442376 | tf_op jit(solution)/shard_map/ppermute | solution.py:26
  55.0 12.0 %collective-permute-start.15 = (f32[3,64,256]{2,1,0:T(8,128)S(1)}, f32[3,64,256]{2,1,0:T(8,128)S(1)}, u32[]{:S(2)}, u32[]{:S(2)}) collective-permute-start(f32[3,64,256]{2,1,0:T(8,128)S(1)} %shard_map.86.refs_3_), channel_id=1, source_target_pairs={{0,2},{2,0},{1,3},{3,1},{4,6},{6,4},{5,7},{7,5},{8,10},{10,8},{9,1... | collective-permute-start | bytes 589832 | tf_op jit(solution)/shard_map/ppermute | solution.py:26
  56.5 10.5 %collective-permute-start.13 = (f32[3,64,256]{2,1,0:T(8,128)S(1)}, f32[3,64,256]{2,1,0:T(8,128)S(1)}, u32[]{:S(2)}, u32[]{:S(2)}) collective-permute-start(f32[3,64,256]{2,1,0:T(8,128)S(1)} %shard_map.83.refs_0_), channel_id=1, source_target_pairs={{0,2},{2,0},{1,3},{3,1},{4,6},{6,4},{5,7},{7,5},{8,10},{10,8},{9,1... | collective-permute-start | bytes 589832 | tf_op jit(solution)/shard_map/ppermute | solution.py:26
  58.3 12.9 %collective-permute-start.17 = (f32[3,64,256]{2,1,0:T(8,128)S(1)}, f32[3,64,256]{2,1,0:T(8,128)S(1)}, u32[]{:S(2)}, u32[]{:S(2)}) collective-permute-start(f32[3,64,256]{2,1,0:T(8,128)S(1)} %shard_map.89.refs_6_), channel_id=1, source_target_pairs={{0,2},{2,0},{1,3},{3,1},{4,6},{6,4},{5,7},{7,5},{8,10},{10,8},{9,1... | collective-permute-start | bytes 589832 | tf_op jit(solution)/shard_map/ppermute | solution.py:26
  62.4 10.9 %collective-permute-start.11 = (f32[3,32,256]{2,1,0:T(8,128)S(1)}, f32[3,32,256]{2,1,0:T(8,128)S(1)}, u32[]{:S(2)}, u32[]{:S(2)}) collective-permute-start(f32[3,32,256]{2,1,0:T(8,128)S(1)} %shard_map.80.refs_2_), channel_id=1, source_target_pairs={{0,2},{2,0},{1,3},{3,1},{4,6},{6,4},{5,7},{7,5},{8,10},{10,8},{9,1... | collective-permute-start | bytes 294920 | tf_op jit(solution)/shard_map/ppermute | solution.py:26
  63.9 10.9 %collective-permute-start.8 = (f32[3,32,256]{2,1,0:T(8,128)S(1)}, f32[3,32,256]{2,1,0:T(8,128)S(1)}, u32[]{:S(2)}, u32[]{:S(2)}) collective-permute-start(f32[3,32,256]{2,1,0:T(8,128)S(1)} %shard_map.78.refs_0_), channel_id=1, source_target_pairs={{0,2},{2,0},{1,3},{3,1},{4,6},{6,4},{5,7},{7,5},{8,10},{10,8},{9,1... | collective-permute-start | bytes 294920 | tf_op jit(solution)/shard_map/ppermute | solution.py:26
  71.2 3.6 %copy-start.3 = (bf16[384,768]{1,0:T(8,128)(2,1)S(1)}, bf16[384,768]{1,0:T(8,128)(2,1)}, u32[]{:S(2)}) copy-start(bf16[384,768]{1,0:T(8,128)(2,1)} %w_out.1) | copy-start | bytes 1769476
  75.7 2.1 %collective-permute-start.23 = (bf16[6,128,384]{2,1,0:T(8,128)(2,1)S(1)}, bf16[6,128,384]{2,1,0:T(8,128)(2,1)S(1)}, u32[]{:S(2)}, u32[]{:S(2)}) collective-permute-start(bf16[6,128,384]{2,1,0:T(8,128)(2,1)S(1)} %get-tuple-element.30), channel_id=1, source_target_pairs={{0,1},{1,0},{2,3},{3,2},{4,5},{5,4},{6,7},{7,6},{8,9},{9,8},{10,11... | collective-permute-start | bytes 1769480 | tf_op jit(solution)/shard_map/ppermute | solution.py:26

commit v2 on v1

--- a/solution.py
+++ b/solution.py
@@ -14,7 +14,7 @@
 PER_TILE = LANES // HEAD_DIM
 CHUNKS = 2
 MARK_ROWS = 8
-CLOSED = 0
+CLOSED = 128
 PIECE = 32
 PARTS = HEAD_DIM // PIECE
 MASKED = -1000000000.0
@@ -31,7 +31,7 @@
     stops = list(range(length))
     if math.prod(lax.axis_size(axis) for axis in ("grp", "res", "seq", "head")) < CLOSED:
         stops = stops[::2] + stops[1::2][::-1]
-    return lax.ppermute(value, "res", [(stops[i - 1], stops[i]) for i in range(length)])
+    return lax.ppermute(value, "res", [(stops[i], stops[i - 1]) for i in range(length)])
 
 
 def whole(count):
@@ -142,10 +142,10 @@
     return piece[piece.shape[0] - MARK_ROWS :].astype(jnp.float32)
 
 
-def project_kernel(query, w_key, w_value, *refs, order, masked):
+def project_kernel(query, w_key, w_value, marks, *refs, order, masked):
     pieces, (logits, values) = refs[:-2], refs[-2:]
     per_chunk = len(pieces) // len(order)
-    marks = marks_of(pieces[0])
+    marks = marks_of(marks)
     for at, chunk in enumerate(order):
         flat = unpack(pieces[at * per_chunk : (at + 1) * per_chunk], w_key.shape[0])
         keys = project(flat, w_key)
@@ -434,9 +434,9 @@
 
     for step, taken in batches(blocks):
         count = len(taken)
-        if count > 1 or cores == 1:
+        if step < last or cores == 1:
             outs = [logits_shape(count * part), values_shape(count)]
-            args = [query, w_key, w_value] + sum([pieces[step, k] for k in taken], [])
+            args = [query, w_key, w_value, moved[step]] + sum([pieces[step, k] for k in taken], [])
             function = functools.partial(project_kernel, order=taken, masked=masked)
             logits, values = kernel(function, outs, args, 2 * count * width * rows)
             units.append(([exchange(logits)], values))

time: 78.9 us -> 86.6 us (1.098)
  starting transfers between devices: 17.1 us -> 24.5 us
  waiting for transfers between devices: 42.1 us -> 44.6 us
  Pallas kernels: 18.2 us -> 16.1 us
    ppermute x7, starting transfers between devices: 4.8 us -> 12.6 us  [pass_on(): lax.ppermute(value, 'res', [(stops[i], stops[i - 1]) for i in range(lengt...]
    ppermute x17, waiting for transfers between devices: 9.89 us -> 14.7 us  [ring(): lax.ppermute(value, axis, [(i, (i + by) % length) for i in range(length)])]
    ppermute x7, waiting for transfers between devices: 32.2 us -> 29.9 us  [pass_on(): lax.ppermute(value, 'res', [(stops[i], stops[i - 1]) for i in range(lengt...]
    pallas_call x26 -> x18, Pallas kernels: 16 us -> 14 us  [call(): pl.pallas_call(kernel, out_shape=out_shape, in_specs=specs, out_specs=who...]
  transfers between devices with their start and end apart: 24 -> 24, of which waited for: 12 -> 13; matrix products, arithmetic and copies ran while one was open for 0% -> 0% of each run, Pallas kernels for 21% -> 16%
where the time goes in v2:
time: 86.6 us; the launch traced here: 86.5 us
  waiting for transfers between devices  44.6 us (52%)
  starting transfers between devices  24.5 us (28%)
  Pallas kernels  16.1 us (19%)
  other arithmetic  0.93 us (1%)
    ppermute x7, waiting for transfers between devices, pass_on(): lax.ppermute(value, 'res', [(stops[i], stops[i - 1]) for i in range(lengt...  29.9 us
    ppermute x17, waiting for transfers between devices, ring(): lax.ppermute(value, axis, [(i, (i + by) % length) for i in range(length)])  14.7 us
    pallas_call x18, Pallas kernels, call(): pl.pallas_call(kernel, out_shape=out_shape, in_specs=specs, out_specs=who...  14 us
    ppermute x7, starting transfers between devices, pass_on(): lax.ppermute(value, 'res', [(stops[i], stops[i - 1]) for i in range(lengt...  12.6 us
    ppermute x17, starting transfers between devices, ring(): lax.ppermute(value, axis, [(i, (i + by) % length) for i in range(length)])  11.9 us
    pallas_call x2, Pallas kernels, shards(): pl.pallas_call(functools.partial(pack_kernel, chunk=k, share=share), out_...  2.16 us
  transfers between devices with their start and end apart: 24, of which 13 were waited for; matrix products, arithmetic and copies ran while one was open for 0% of the time, Pallas kernels for 16%

profile of v2, /device:TPU:0, one launch (start us, length us, event | category | flops | bytes accessed | tf_op | source)
XLA Modules:
  0.0 86.5 jit_solution(2926458808201198849)
XLA Ops:
  0.0 1.1 %shard_map.74 = bf16[1160,128]{1,0:T(8,128)(2,1)S(1)} custom-call(bf16[6,128,768]{2,1,0:T(8,128)(2,1)} %tokens.3, s32[1,128]{1,0:T(1,128)} %bitcast.1), custom_call_target="tpu_custom_call" | custom-call | tf_op jit(solution)/shard_map/pallas_call | solution.py:356
  1.1 0.0 copy-start
  1.2 0.0 copy-start.1
  1.2 0.0 copy-start.4
  1.2 0.0 copy-start.5
  1.2 3.1 %collective-permute-start.1 = (bf16[1160,128]{1,0:T(8,128)(2,1)S(1)}, bf16[1160,128]{1,0:T(8,128)(2,1)S(1)}, u32[]{:S(2)}, u32[]{:S(2)}) collective-permute-start(bf16[1160,128]{1,0:T(8,128)(2,1)S(1)} %shard_map.74), channel_id=1, source_target_pairs={{0,4},{8,0},{12,8},{4,12},{1,5},{9,1},{13,9},{5,13},{2,6},{10,2},{... | collective-permute-start | bytes 890888 | tf_op jit(solution)/shard_map/ppermute | solution.py:34
  4.3 8.1 %collective-permute-done.1.marks.refs_0_ = bf16[1160,128]{1,0:T(8,128)(2,1)S(1)} collective-permute-done((bf16[1160,128]{1,0:T(8,128)(2,1)S(1)}, bf16[1160,128]{1,0:T(8,128)(2,1)S(1)}, u32[]{:S(2)}, u32[]{:S(2)}) %collective-permute-start.1) | collective-permute-done | bytes 296992 | tf_op jit(solution)/shard_map/ppermute | solution.py:34
  12.4 0.8 collective-permute-start.2
  13.2 1.0 %shard_map.75 = bf16[1152,128]{1,0:T(8,128)(2,1)S(1)} custom-call(bf16[6,128,768]{2,1,0:T(8,128)(2,1)} %tokens.3, s32[1,128]{1,0:T(1,128)} %bitcast.2), custom_call_target="tpu_custom_call" | custom-call | tf_op jit(solution)/shard_map/pallas_call | solution.py:356
  14.2 3.4 %collective-permute-start.4 = (bf16[1152,128]{1,0:T(8,128)(2,1)S(1)}, bf16[1152,128]{1,0:T(8,128)(2,1)S(1)}, u32[]{:S(2)}, u32[]{:S(2)}) collective-permute-start(bf16[1152,128]{1,0:T(8,128)(2,1)S(1)} %shard_map.75), channel_id=1, source_target_pairs={{0,4},{8,0},{12,8},{4,12},{1,5},{9,1},{13,9},{5,13},{2,6},{10,2},{... | collective-permute-start | bytes 884744 | tf_op jit(solution)/shard_map/ppermute | solution.py:34
  17.7 5.5 %collective-permute-done.2.marks.refs_0_ = bf16[1160,128]{1,0:T(8,128)(2,1)S(1)} collective-permute-done((bf16[1160,128]{1,0:T(8,128)(2,1)S(1)}, bf16[1160,128]{1,0:T(8,128)(2,1)S(1)}, u32[]{:S(2)}, u32[]{:S(2)}) %collective-permute-start.2) | collective-permute-done | bytes 296992 | tf_op jit(solution)/shard_map/ppermute | solution.py:34
  23.2 0.8 collective-permute-start.3
  24.0 5.5 %collective-permute-done.4.refs_0_ = bf16[1152,128]{1,0:T(8,128)(2,1)S(1)} collective-permute-done((bf16[1152,128]{1,0:T(8,128)(2,1)S(1)}, bf16[1152,128]{1,0:T(8,128)(2,1)S(1)}, u32[]{:S(2)}, u32[]{:S(2)}) %collective-permute-start.4) | collective-permute-done | bytes 294944 | tf_op jit(solution)/shard_map/ppermute | solution.py:34
  29.5 0.8 collective-permute-start.5
  30.3 0.5 collective-permute-start.19
  30.9 1.5 %collective-permute-start = (s32[6]{0:T(128)S(1)}, s32[6]{0:T(128)S(1)}, u32[]{:S(2)}, u32[]{:S(2)}) collective-permute-start(s32[6]{0:T(128)S(1)} %copy-done.6), channel_id=1, source_target_pairs={{0,2},{2,0},{1,3},{3,1},{4,6},{6,4},{5,7},{7,5},{8,10},{10,8},{9,1... | collective-permute-start | bytes 80 | tf_op jit(solution)/shard_map/ppermute | solution.py:26
  32.3 8.1 %collective-permute-done.5.packed.refs_0_ = bf16[1152,128]{1,0:T(8,128)(2,1)S(1)} collective-permute-done((bf16[1152,128]{1,0:T(8,128)(2,1)S(1)}, bf16[1152,128]{1,0:T(8,128)(2,1)S(1)}, u32[]{:S(2)}, u32[]{:S(2)}) %collective-permute-start.5) | collective-permute-done | bytes 294944 | tf_op jit(solution)/shard_map/ppermute | solution.py:34
  40.5 0.6 collective-permute-start.9
  41.1 0.0 collective-permute-done.refs_1_
  41.1 0.5 collective-permute-start.12
  41.6 0.0 collective-permute-done.3.marks.piece.refs_0_
  41.6 0.1 collective-permute-start.16
  41.7 2.9 %shard_map.73 = (bf16[3,256,768]{2,1,0:T(8,128)(2,1)S(1)}, f32[3,128,256]{2,1,0:T(8,128)S(1)}, bf16[2,3,128,768]{3,2,1,0:T(8,128)(2,1)S(1)}) custom-call(s32[6]{0:T(128)S(1)} %copy-done.6, s32[6]{0:T(128)S(1)} %collective-permute-done.refs_1_, s32[1,128]{1,0:T(1,128)S(1)} %bitcast.3, bf16[6,128,768]{2,1,0:T(8,128)(2,1)S(1)} %copy-done.2, ...), custom_call_target="tpu_custom_call" | custom-call | flops 1509949440 | bytes 2949680 | tf_op jit(solution)/shard_map/pallas_call | solution.py:45
  44.6 0.0 collective-permute-done.19.refs_1_
  44.6 1.6 %collective-permute-start.18 = (f32[3,128,256]{2,1,0:T(8,128)S(1)}, f32[3,128,256]{2,1,0:T(8,128)S(1)}, u32[]{:S(2)}, u32[]{:S(2)}) collective-permute-start(f32[3,128,256]{2,1,0:T(8,128)S(1)} %get-tuple-element.33.refs_0_), channel_id=1, source_target_pairs={{0,2},{2,0},{1,3},{3,1},{4,6},{6,4},{5,7},{7,5},{8,10},{10,8},{9,1... | collective-permute-start | bytes 1179656 | tf_op jit(solution)/shard_map/ppermute | solution.py:26
  46.2 0.4 collective-permute-done.9.piece.refs_2_
  46.6 3.0 %collective-permute-start.6 = (bf16[576,128]{1,0:T(8,128)(2,1)S(1)}, bf16[576,128]{1,0:T(8,128)(2,1)S(1)}, u32[]{:S(2)}, u32[]{:S(2)}) collective-permute-start(bf16[576,128]{1,0:T(8,128)(2,1)S(1)} %get-tuple-element.27), channel_id=1, source_target_pairs={{0,4},{8,0},{12,8},{4,12},{1,5},{9,1},{13,9},{5,13},{2,6},{10,2},{... | collective-permute-start | bytes 442376 | tf_op jit(solution)/shard_map/ppermute | solution.py:34
  49.6 1.1 %shard_map.88 = (f32[3,64,256]{2,1,0:T(8,128)S(1)}, bf16[1,3,128,768]{3,2,1,0:T(8,128)(2,1)S(1)}) custom-call(bf16[3,256,768]{2,1,0:T(8,128)(2,1)S(1)} %get-tuple-element.26.query, bf16[768,384]{1,0:T(8,128)(2,1)S(1)} %copy-done, bf16[768,384]{1,0:T(8,128)(2,1)S(1)} %copy-done.1, bf16[1160,128]{1,0:T(8,128)(2,1)S(1)} %collective-permute-done.1.marks.refs_0_, ...), custom_call_target="tpu_custom_call" | custom-call | flops 452984832 | bytes 3246080 | tf_op jit(solution)/shard_map/pallas_call | solution.py:45
  50.7 2.3 %collective-permute-done.6.piece.refs_0_ = bf16[576,128]{1,0:T(8,128)(2,1)S(1)} collective-permute-done((bf16[576,128]{1,0:T(8,128)(2,1)S(1)}, bf16[576,128]{1,0:T(8,128)(2,1)S(1)}, u32[]{:S(2)}, u32[]{:S(2)}) %collective-permute-start.6) | collective-permute-done | bytes 147488 | tf_op jit(solution)/shard_map/ppermute | solution.py:34
  53.0 0.5 collective-permute-start.7
  53.5 1.1 %shard_map.87 = (f32[3,64,256]{2,1,0:T(8,128)S(1)}, bf16[1,3,128,768]{3,2,1,0:T(8,128)(2,1)S(1)}) custom-call(bf16[3,256,768]{2,1,0:T(8,128)(2,1)S(1)} %get-tuple-element.26.query, bf16[768,384]{1,0:T(8,128)(2,1)S(1)} %copy-done, bf16[768,384]{1,0:T(8,128)(2,1)S(1)} %copy-done.1, bf16[1160,128]{1,0:T(8,128)(2,1)S(1)} %collective-permute-done.1.marks.refs_0_, ...), custom_call_target="tpu_custom_call" | custom-call | flops 452984832 | bytes 3250176 | tf_op jit(solution)/shard_map/pallas_call | solution.py:45
  54.7 1.0 %collective-permute-start.22 = (f32[3,64,256]{2,1,0:T(8,128)S(1)}, f32[3,64,256]{2,1,0:T(8,128)S(1)}, u32[]{:S(2)}, u32[]{:S(2)}) collective-permute-start(f32[3,64,256]{2,1,0:T(8,128)S(1)} %get-tuple-element.37.refs_6_), channel_id=1, source_target_pairs={{0,2},{2,0},{1,3},{3,1},{4,6},{6,4},{5,7},{7,5},{8,10},{10,8},{9,1... | collective-permute-start | bytes 589832 | tf_op jit(solution)/shard_map/ppermute | solution.py:26
  55.6 0.0 collective-permute-done.16.refs_0_.refs_1_
  55.6 1.1 %collective-permute-start.20 = (f32[3,64,256]{2,1,0:T(8,128)S(1)}, f32[3,64,256]{2,1,0:T(8,128)S(1)}, u32[]{:S(2)}, u32[]{:S(2)}) collective-permute-start(f32[3,64,256]{2,1,0:T(8,128)S(1)} %get-tuple-element.35.refs_3_), channel_id=1, source_target_pairs={{0,2},{2,0},{1,3},{3,1},{4,6},{6,4},{5,7},{7,5},{8,10},{10,8},{9,1... | collective-permute-start | bytes 589832 | tf_op jit(solution)/shard_map/ppermute | solution.py:26
  56.8 1.1 %shard_map.83 = (f32[3,64,256]{2,1,0:T(8,128)S(1)}, bf16[1,3,128,768]{3,2,1,0:T(8,128)(2,1)S(1)}) custom-call(bf16[3,256,768]{2,1,0:T(8,128)(2,1)S(1)} %get-tuple-element.26.query, bf16[768,384]{1,0:T(8,128)(2,1)S(1)} %copy-done, bf16[768,384]{1,0:T(8,128)(2,1)S(1)} %copy-done.1, bf16[1160,128]{1,0:T(8,128)(2,1)S(1)} %collective-permute-done.2.marks.refs_0_, ...), custom_call_target="tpu_custom_call" | custom-call | flops 452984832 | bytes 3246080 | tf_op jit(solution)/shard_map/pallas_call | solution.py:45
  57.9 0.6 shard_map.84.before
  58.5 1.1 %shard_map.82 = (f32[3,64,256]{2,1,0:T(8,128)S(1)}, bf16[1,3,128,768]{3,2,1,0:T(8,128)(2,1)S(1)}) custom-call(bf16[3,256,768]{2,1,0:T(8,128)(2,1)S(1)} %get-tuple-element.26.query, bf16[768,384]{1,0:T(8,128)(2,1)S(1)} %copy-done, bf16[768,384]{1,0:T(8,128)(2,1)S(1)} %copy-done.1, bf16[1160,128]{1,0:T(8,128)(2,1)S(1)} %collective-permute-done.2.marks.refs_0_, ...), custom_call_target="tpu_custom_call" | custom-call | flops 452984832 | bytes 3250176 | tf_op jit(solution)/shard_map/pallas_call | solution.py:45
  59.6 0.6 shard_map.85.refs_6_
  60.2 1.0 %collective-permute-start.15 = (f32[3,64,256]{2,1,0:T(8,128)S(1)}, f32[3,64,256]{2,1,0:T(8,128)S(1)}, u32[]{:S(2)}, u32[]{:S(2)}) collective-permute-start(f32[3,64,256]{2,1,0:T(8,128)S(1)} %get-tuple-element.31.refs_3_), channel_id=1, source_target_pairs={{0,2},{2,0},{1,3},{3,1},{4,6},{6,4},{5,7},{7,5},{8,10},{10,8},{9,1... | collective-permute-start | bytes 589832 | tf_op jit(solution)/shard_map/ppermute | solution.py:26
  61.2 0.0 collective-permute-done.10.refs_0_.refs_3_
  61.2 1.1 %collective-permute-start.13 = (f32[3,64,256]{2,1,0:T(8,128)S(1)}, f32[3,64,256]{2,1,0:T(8,128)S(1)}, u32[]{:S(2)}, u32[]{:S(2)}) collective-permute-start(f32[3,64,256]{2,1,0:T(8,128)S(1)} %get-tuple-element.29.refs_0_), channel_id=1, source_target_pairs={{0,2},{2,0},{1,3},{3,1},{4,6},{6,4},{5,7},{7,5},{8,10},{10,8},{9,1... | collective-permute-start | bytes 589832 | tf_op jit(solution)/shard_map/ppermute | solution.py:26
  62.3 0.9 %collective-permute-start.17 = (f32[3,64,256]{2,1,0:T(8,128)S(1)}, f32[3,64,256]{2,1,0:T(8,128)S(1)}, u32[]{:S(2)}, u32[]{:S(2)}) collective-permute-start(f32[3,64,256]{2,1,0:T(8,128)S(1)} %shard_map.85.refs_6_), channel_id=1, source_target_pairs={{0,2},{2,0},{1,3},{3,1},{4,6},{6,4},{5,7},{7,5},{8,10},{10,8},{9,1... | collective-permute-start | bytes 589832 | tf_op jit(solution)/shard_map/ppermute | solution.py:26
  63.2 0.5 shard_map.79.before
  63.7 0.5 shard_map.77.before
  64.1 0.5 shard_map.80.refs_2_
  64.6 0.5 shard_map.78.refs_0_
  65.1 0.0 collective-permute-done.22.refs_7_
  65.1 1.2 %collective-permute-start.11 = (f32[3,32,256]{2,1,0:T(8,128)S(1)}, f32[3,32,256]{2,1,0:T(8,128)S(1)}, u32[]{:S(2)}, u32[]{:S(2)}) collective-permute-start(f32[3,32,256]{2,1,0:T(8,128)S(1)} %shard_map.80.refs_2_), channel_id=1, source_target_pairs={{0,2},{2,0},{1,3},{3,1},{4,6},{6,4},{5,7},{7,5},{8,10},{10,8},{9,1... | collective-permute-start | bytes 294920 | tf_op jit(solution)/shard_map/ppermute | solution.py:26
  66.3 0.4 collective-permute-done.20.refs_4_
  66.7 0.9 %collective-permute-start.8 = (f32[3,32,256]{2,1,0:T(8,128)S(1)}, f32[3,32,256]{2,1,0:T(8,128)S(1)}, u32[]{:S(2)}, u32[]{:S(2)}) collective-permute-start(f32[3,32,256]{2,1,0:T(8,128)S(1)} %shard_map.78.refs_0_), channel_id=1, source_target_pairs={{0,2},{2,0},{1,3},{3,1},{4,6},{6,4},{5,7},{7,5},{8,10},{10,8},{9,1... | collective-permute-start | bytes 294920 | tf_op jit(solution)/shard_map/ppermute | solution.py:26
  67.6 0.6 shard_map.89
  68.2 0.5 shard_map.81.refs_4_
  68.7 0.5 shard_map.86.refs_8_
  69.2 1.7 %collective-permute-done.15.refs_4_ = f32[3,64,256]{2,1,0:T(8,128)S(1)} collective-permute-done((f32[3,64,256]{2,1,0:T(8,128)S(1)}, f32[3,64,256]{2,1,0:T(8,128)S(1)}, u32[]{:S(2)}, u32[]{:S(2)}) %collective-permute-start.15) | collective-permute-done | bytes 196640 | tf_op jit(solution)/shard_map/ppermute | solution.py:26
  70.9 4.2 %collective-permute-done.13.refs_1_ = f32[3,64,256]{2,1,0:T(8,128)S(1)} collective-permute-done((f32[3,64,256]{2,1,0:T(8,128)S(1)}, f32[3,64,256]{2,1,0:T(8,128)S(1)}, u32[]{:S(2)}, u32[]{:S(2)}) %collective-permute-start.13) | collective-permute-done | bytes 196640 | tf_op jit(solution)/shard_map/ppermute | solution.py:26
  75.1 4.2 %collective-permute-done.17.refs_7_ = f32[3,64,256]{2,1,0:T(8,128)S(1)} collective-permute-done((f32[3,64,256]{2,1,0:T(8,128)S(1)}, f32[3,64,256]{2,1,0:T(8,128)S(1)}, u32[]{:S(2)}, u32[]{:S(2)}) %collective-permute-start.17) | collective-permute-done | bytes 196640 | tf_op jit(solution)/shard_map/ppermute | solution.py:26
  79.4 0.6 shard_map.90
  79.9 1.5 %collective-permute-done.11.refs_3_ = f32[3,32,256]{2,1,0:T(8,128)S(1)} collective-permute-done((f32[3,32,256]{2,1,0:T(8,128)S(1)}, f32[3,32,256]{2,1,0:T(8,128)S(1)}, u32[]{:S(2)}, u32[]{:S(2)}) %collective-permute-start.11) | collective-permute-done | bytes 98336 | tf_op jit(solution)/shard_map/ppermute | solution.py:26
  81.5 1.2 %collective-permute-done.8.refs_1_ = f32[3,32,256]{2,1,0:T(8,128)S(1)} collective-permute-done((f32[3,32,256]{2,1,0:T(8,128)S(1)}, f32[3,32,256]{2,1,0:T(8,128)S(1)}, u32[]{:S(2)}, u32[]{:S(2)}) %collective-permute-start.8) | collective-permute-done | bytes 98336 | tf_op jit(solution)/shard_map/ppermute | solution.py:26
  82.6 0.9 shard_map.91
  83.5 0.1 collective-permute-start.23
  83.6 0.5 shard_map.92
  84.1 1.4 %collective-permute-done.23 = bf16[6,128,384]{2,1,0:T(8,128)(2,1)S(1)} collective-permute-done((bf16[6,128,384]{2,1,0:T(8,128)(2,1)S(1)}, bf16[6,128,384]{2,1,0:T(8,128)(2,1)S(1)}, u32[]{:S(2)}, u32[]{:S(2)}) %collective-permute-start.23) | collective-permute-done | bytes 589856 | tf_op jit(solution)/shard_map/ppermute | solution.py:26
  85.5 0.9 %add_convert_fusion = bf16[6,128,384]{2,1,0:T(8,128)(2,1)} fusion(f32[6,128,384]{2,1,0:T(8,128)S(1)} %shard_map.92, bf16[6,128,384]{2,1,0:T(8,128)(2,1)S(1)} %collective-permute-done.23), kind=kLoop, calls=%fused_computation | loop fusion | flops 884736 | bytes 2359296 | tf_op jit(solution)/shard_map/convert_element_type | solution.py:508
  (19 shorter events, 0.1 us)
Async XLA Ops:
  0.0 30.9 %copy-start.6 = (s32[6]{0:T(128)S(1)}, s32[6]{0:T(128)}, u32[]{:S(2)}) copy-start(s32[6]{0:T(128)} %refs_0_.1) | copy-start | bytes 76
  0.0 41.7 %copy-start.2 = (bf16[6,128,768]{2,1,0:T(8,128)(2,1)S(1)}, bf16[6,128,768]{2,1,0:T(8,128)(2,1)}, u32[]{:S(2)}) copy-start(bf16[6,128,768]{2,1,0:T(8,128)(2,1)} %tokens.3) | copy-start | bytes 3538948
  1.1 40.6 %copy-start = (bf16[768,384]{1,0:T(8,128)(2,1)S(1)}, bf16[768,384]{1,0:T(8,128)(2,1)}, u32[]{:S(2)}) copy-start(bf16[768,384]{1,0:T(8,128)(2,1)} %w_key.19) | copy-start | bytes 1769476
  1.2 40.6 %copy-start.1 = (bf16[768,384]{1,0:T(8,128)(2,1)S(1)}, bf16[768,384]{1,0:T(8,128)(2,1)}, u32[]{:S(2)}) copy-start(bf16[768,384]{1,0:T(8,128)(2,1)} %w_value.11) | copy-start | bytes 1769476
  1.2 40.5 %copy-start.4 = (s32[128]{0:T(128)S(1)}, s32[128]{0:T(128)}, u32[]{:S(2)}) copy-start(s32[128]{0:T(128)} %param.9) | copy-start | bytes 1540
  1.2 40.5 %copy-start.5 = (bf16[768,384]{1,0:T(8,128)(2,1)S(1)}, bf16[768,384]{1,0:T(8,128)(2,1)}, u32[]{:S(2)}) copy-start(bf16[768,384]{1,0:T(8,128)(2,1)} %refs_4_.1) | copy-start | bytes 1769476
  1.2 11.2 %collective-permute-start.1 = (bf16[1160,128]{1,0:T(8,128)(2,1)S(1)}, bf16[1160,128]{1,0:T(8,128)(2,1)S(1)}, u32[]{:S(2)}, u32[]{:S(2)}) collective-permute-start(bf16[1160,128]{1,0:T(8,128)(2,1)S(1)} %shard_map.74), channel_id=1, source_target_pairs={{0,4},{8,0},{12,8},{4,12},{1,5},{9,1},{13,9},{5,13},{2,6},{10,2},{... | collective-permute-start | bytes 890888 | tf_op jit(solution)/shard_map/ppermute | solution.py:34
  12.4 10.8 %collective-permute-start.2 = (bf16[1160,128]{1,0:T(8,128)(2,1)S(1)}, bf16[1160,128]{1,0:T(8,128)(2,1)S(1)}, u32[]{:S(2)}, u32[]{:S(2)}) collective-permute-start(bf16[1160,128]{1,0:T(8,128)(2,1)S(1)} %collective-permute-done.1.marks.refs_0_), channel_id=1, source_target_pairs={{0,4},{8,0},{12,8},{4,12},{1,5},{9,1},{13,9},{5,13},{2,6},{10,2},{... | collective-permute-start | bytes 890888 | tf_op jit(solution)/shard_map/ppermute | solution.py:34
  14.2 15.3 %collective-permute-start.4 = (bf16[1152,128]{1,0:T(8,128)(2,1)S(1)}, bf16[1152,128]{1,0:T(8,128)(2,1)S(1)}, u32[]{:S(2)}, u32[]{:S(2)}) collective-permute-start(bf16[1152,128]{1,0:T(8,128)(2,1)S(1)} %shard_map.75), channel_id=1, source_target_pairs={{0,4},{8,0},{12,8},{4,12},{1,5},{9,1},{13,9},{5,13},{2,6},{10,2},{... | collective-permute-start | bytes 884744 | tf_op jit(solution)/shard_map/ppermute | solution.py:34
  23.2 18.5 %collective-permute-start.3 = (bf16[1160,128]{1,0:T(8,128)(2,1)S(1)}, bf16[1160,128]{1,0:T(8,128)(2,1)S(1)}, u32[]{:S(2)}, u32[]{:S(2)}) collective-permute-start(bf16[1160,128]{1,0:T(8,128)(2,1)S(1)} %collective-permute-done.2.marks.refs_0_), channel_id=1, source_target_pairs={{0,4},{8,0},{12,8},{4,12},{1,5},{9,1},{13,9},{5,13},{2,6},{10,2},{... | collective-permute-start | bytes 890888 | tf_op jit(solution)/shard_map/ppermute | solution.py:34
  29.5 11.0 %collective-permute-start.5 = (bf16[1152,128]{1,0:T(8,128)(2,1)S(1)}, bf16[1152,128]{1,0:T(8,128)(2,1)S(1)}, u32[]{:S(2)}, u32[]{:S(2)}) collective-permute-start(bf16[1152,128]{1,0:T(8,128)(2,1)S(1)} %collective-permute-done.4.refs_0_), channel_id=1, source_target_pairs={{0,4},{8,0},{12,8},{4,12},{1,5},{9,1},{13,9},{5,13},{2,6},{10,2},{... | collective-permute-start | bytes 884744 | tf_op jit(solution)/shard_map/ppermute | solution.py:34
  30.3 10.8 %collective-permute-start.21 = (bf16[1152,128]{1,0:T(8,128)(2,1)S(1)}, bf16[1152,128]{1,0:T(8,128)(2,1)S(1)}, u32[]{:S(2)}, u32[]{:S(2)}) collective-permute-start(bf16[1152,128]{1,0:T(8,128)(2,1)S(1)} %collective-permute-done.4.refs_0_), channel_id=1, source_target_pairs={{0,1},{1,0},{2,3},{3,2},{4,5},{5,4},{6,7},{7,6},{8,9},{9,8},{10,11... | collective-permute-start | bytes 884744 | tf_op jit(solution)/shard_map/ppermute | solution.py:26
  30.3 14.3 %collective-permute-start.19 = (bf16[1160,128]{1,0:T(8,128)(2,1)S(1)}, bf16[1160,128]{1,0:T(8,128)(2,1)S(1)}, u32[]{:S(2)}, u32[]{:S(2)}) collective-permute-start(bf16[1160,128]{1,0:T(8,128)(2,1)S(1)} %collective-permute-done.1.marks.refs_0_), channel_id=1, source_target_pairs={{0,1},{1,0},{2,3},{3,2},{4,5},{5,4},{6,7},{7,6},{8,9},{9,8},{10,11... | collective-permute-start | bytes 890888 | tf_op jit(solution)/shard_map/ppermute | solution.py:26
  30.9 10.3 %collective-permute-start = (s32[6]{0:T(128)S(1)}, s32[6]{0:T(128)S(1)}, u32[]{:S(2)}, u32[]{:S(2)}) collective-permute-start(s32[6]{0:T(128)S(1)} %copy-done.6), channel_id=1, source_target_pairs={{0,2},{2,0},{1,3},{3,1},{4,6},{6,4},{5,7},{7,5},{8,10},{10,8},{9,1... | collective-permute-start | bytes 80 | tf_op jit(solution)/shard_map/ppermute | solution.py:26
  40.5 6.1 %collective-permute-start.9 = (bf16[576,128]{1,0:T(8,128)(2,1)S(1)}, bf16[576,128]{1,0:T(8,128)(2,1)S(1)}, u32[]{:S(2)}, u32[]{:S(2)}) collective-permute-start(bf16[576,128]{1,0:T(8,128)(2,1)S(1)} %get-tuple-element.28), channel_id=1, source_target_pairs={{0,4},{8,0},{12,8},{4,12},{1,5},{9,1},{13,9},{5,13},{2,6},{10,2},{... | collective-permute-start | bytes 442376 | tf_op jit(solution)/shard_map/ppermute | solution.py:34
  41.1 11.9 %collective-permute-start.14 = (bf16[1152,128]{1,0:T(8,128)(2,1)S(1)}, bf16[1152,128]{1,0:T(8,128)(2,1)S(1)}, u32[]{:S(2)}, u32[]{:S(2)}) collective-permute-start(bf16[1152,128]{1,0:T(8,128)(2,1)S(1)} %collective-permute-done.5.packed.refs_0_), channel_id=1, source_target_pairs={{0,1},{1,0},{2,3},{3,2},{4,5},{5,4},{6,7},{7,6},{8,9},{9,8},{10,11... | collective-permute-start | bytes 884744 | tf_op jit(solution)/shard_map/ppermute | solution.py:26
  41.1 13.5 %collective-permute-start.12 = (bf16[1160,128]{1,0:T(8,128)(2,1)S(1)}, bf16[1160,128]{1,0:T(8,128)(2,1)S(1)}, u32[]{:S(2)}, u32[]{:S(2)}) collective-permute-start(bf16[1160,128]{1,0:T(8,128)(2,1)S(1)} %collective-permute-done.2.marks.refs_0_), channel_id=1, source_target_pairs={{0,1},{1,0},{2,3},{3,2},{4,5},{5,4},{6,7},{7,6},{8,9},{9,8},{10,11... | collective-permute-start | bytes 890888 | tf_op jit(solution)/shard_map/ppermute | solution.py:26
  41.6 14.0 %collective-permute-start.16 = (bf16[1160,128]{1,0:T(8,128)(2,1)S(1)}, bf16[1160,128]{1,0:T(8,128)(2,1)S(1)}, u32[]{:S(2)}, u32[]{:S(2)}) collective-permute-start(bf16[1160,128]{1,0:T(8,128)(2,1)S(1)} %collective-permute-done.3.marks.piece.refs_0_), channel_id=1, source_target_pairs={{0,1},{1,0},{2,3},{3,2},{4,5},{5,4},{6,7},{7,6},{8,9},{9,8},{10,11... | collective-permute-start | bytes 890888 | tf_op jit(solution)/shard_map/ppermute | solution.py:26
  44.6 15.6 %collective-permute-start.18 = (f32[3,128,256]{2,1,0:T(8,128)S(1)}, f32[3,128,256]{2,1,0:T(8,128)S(1)}, u32[]{:S(2)}, u32[]{:S(2)}) collective-permute-start(f32[3,128,256]{2,1,0:T(8,128)S(1)} %get-tuple-element.33.refs_0_), channel_id=1, source_target_pairs={{0,2},{2,0},{1,3},{3,1},{4,6},{6,4},{5,7},{7,5},{8,10},{10,8},{9,1... | collective-permute-start | bytes 1179656 | tf_op jit(solution)/shard_map/ppermute | solution.py:26
  46.6 6.4 %collective-permute-start.6 = (bf16[576,128]{1,0:T(8,128)(2,1)S(1)}, bf16[576,128]{1,0:T(8,128)(2,1)S(1)}, u32[]{:S(2)}, u32[]{:S(2)}) collective-permute-start(bf16[576,128]{1,0:T(8,128)(2,1)S(1)} %get-tuple-element.27), channel_id=1, source_target_pairs={{0,4},{8,0},{12,8},{4,12},{1,5},{9,1},{13,9},{5,13},{2,6},{10,2},{... | collective-permute-start | bytes 442376 | tf_op jit(solution)/shard_map/ppermute | solution.py:34
  53.0 8.2 %collective-permute-start.10 = (bf16[576,128]{1,0:T(8,128)(2,1)S(1)}, bf16[576,128]{1,0:T(8,128)(2,1)S(1)}, u32[]{:S(2)}, u32[]{:S(2)}) collective-permute-start(bf16[576,128]{1,0:T(8,128)(2,1)S(1)} %collective-permute-done.9.piece.refs_2_), channel_id=1, source_target_pairs={{0,1},{1,0},{2,3},{3,2},{4,5},{5,4},{6,7},{7,6},{8,9},{9,8},{10,11... | collective-permute-start | bytes 442376 | tf_op jit(solution)/shard_map/ppermute | solution.py:26
  53.0 9.3 %collective-permute-start.7 = (bf16[576,128]{1,0:T(8,128)(2,1)S(1)}, bf16[576,128]{1,0:T(8,128)(2,1)S(1)}, u32[]{:S(2)}, u32[]{:S(2)}) collective-permute-start(bf16[576,128]{1,0:T(8,128)(2,1)S(1)} %collective-permute-done.6.piece.refs_0_), channel_id=1, source_target_pairs={{0,1},{1,0},{2,3},{3,2},{4,5},{5,4},{6,7},{7,6},{8,9},{9,8},{10,11... | collective-permute-start | bytes 442376 | tf_op jit(solution)/shard_map/ppermute | solution.py:26
  54.7 10.5 %collective-permute-start.22 = (f32[3,64,256]{2,1,0:T(8,128)S(1)}, f32[3,64,256]{2,1,0:T(8,128)S(1)}, u32[]{:S(2)}, u32[]{:S(2)}) collective-permute-start(f32[3,64,256]{2,1,0:T(8,128)S(1)} %get-tuple-element.37.refs_6_), channel_id=1, source_target_pairs={{0,2},{2,0},{1,3},{3,1},{4,6},{6,4},{5,7},{7,5},{8,10},{10,8},{9,1... | collective-permute-start | bytes 589832 | tf_op jit(solution)/shard_map/ppermute | solution.py:26
  55.6 11.1 %collective-permute-start.20 = (f32[3,64,256]{2,1,0:T(8,128)S(1)}, f32[3,64,256]{2,1,0:T(8,128)S(1)}, u32[]{:S(2)}, u32[]{:S(2)}) collective-permute-start(f32[3,64,256]{2,1,0:T(8,128)S(1)} %get-tuple-element.35.refs_3_), channel_id=1, source_target_pairs={{0,2},{2,0},{1,3},{3,1},{4,6},{6,4},{5,7},{7,5},{8,10},{10,8},{9,1... | collective-permute-start | bytes 589832 | tf_op jit(solution)/shard_map/ppermute | solution.py:26
  60.2 10.7 %collective-permute-start.15 = (f32[3,64,256]{2,1,0:T(8,128)S(1)}, f32[3,64,256]{2,1,0:T(8,128)S(1)}, u32[]{:S(2)}, u32[]{:S(2)}) collective-permute-start(f32[3,64,256]{2,1,0:T(8,128)S(1)} %get-tuple-element.31.refs_3_), channel_id=1, source_target_pairs={{0,2},{2,0},{1,3},{3,1},{4,6},{6,4},{5,7},{7,5},{8,10},{10,8},{9,1... | collective-permute-start | bytes 589832 | tf_op jit(solution)/shard_map/ppermute | solution.py:26
  61.2 14.0 %collective-permute-start.13 = (f32[3,64,256]{2,1,0:T(8,128)S(1)}, f32[3,64,256]{2,1,0:T(8,128)S(1)}, u32[]{:S(2)}, u32[]{:S(2)}) collective-permute-start(f32[3,64,256]{2,1,0:T(8,128)S(1)} %get-tuple-element.29.refs_0_), channel_id=1, source_target_pairs={{0,2},{2,0},{1,3},{3,1},{4,6},{6,4},{5,7},{7,5},{8,10},{10,8},{9,1... | collective-permute-start | bytes 589832 | tf_op jit(solution)/shard_map/ppermute | solution.py:26
  62.3 17.1 %collective-permute-start.17 = (f32[3,64,256]{2,1,0:T(8,128)S(1)}, f32[3,64,256]{2,1,0:T(8,128)S(1)}, u32[]{:S(2)}, u32[]{:S(2)}) collective-permute-start(f32[3,64,256]{2,1,0:T(8,128)S(1)} %shard_map.85.refs_6_), channel_id=1, source_target_pairs={{0,2},{2,0},{1,3},{3,1},{4,6},{6,4},{5,7},{7,5},{8,10},{10,8},{9,1... | collective-permute-start | bytes 589832 | tf_op jit(solution)/shard_map/ppermute | solution.py:26
  65.1 16.3 %collective-permute-start.11 = (f32[3,32,256]{2,1,0:T(8,128)S(1)}, f32[3,32,256]{2,1,0:T(8,128)S(1)}, u32[]{:S(2)}, u32[]{:S(2)}) collective-permute-start(f32[3,32,256]{2,1,0:T(8,128)S(1)} %shard_map.80.refs_2_), channel_id=1, source_target_pairs={{0,2},{2,0},{1,3},{3,1},{4,6},{6,4},{5,7},{7,5},{8,10},{10,8},{9,1... | collective-permute-start | bytes 294920 | tf_op jit(solution)/shard_map/ppermute | solution.py:26
  66.7 15.9 %collective-permute-start.8 = (f32[3,32,256]{2,1,0:T(8,128)S(1)}, f32[3,32,256]{2,1,0:T(8,128)S(1)}, u32[]{:S(2)}, u32[]{:S(2)}) collective-permute-start(f32[3,32,256]{2,1,0:T(8,128)S(1)} %shard_map.78.refs_0_), channel_id=1, source_target_pairs={{0,2},{2,0},{1,3},{3,1},{4,6},{6,4},{5,7},{7,5},{8,10},{10,8},{9,1... | collective-permute-start | bytes 294920 | tf_op jit(solution)/shard_map/ppermute | solution.py:26
  79.4 3.3 %copy-start.3 = (bf16[384,768]{1,0:T(8,128)(2,1)S(1)}, bf16[384,768]{1,0:T(8,128)(2,1)}, u32[]{:S(2)}) copy-start(bf16[384,768]{1,0:T(8,128)(2,1)} %w_out.1) | copy-start | bytes 1769476
  83.5 2.1 %collective-permute-start.23 = (bf16[6,128,384]{2,1,0:T(8,128)(2,1)S(1)}, bf16[6,128,384]{2,1,0:T(8,128)(2,1)S(1)}, u32[]{:S(2)}, u32[]{:S(2)}) collective-permute-start(bf16[6,128,384]{2,1,0:T(8,128)(2,1)S(1)} %get-tuple-element.46), channel_id=1, source_target_pairs={{0,1},{1,0},{2,3},{3,2},{4,5},{5,4},{6,7},{7,6},{8,9},{9,8},{10,11... | collective-permute-start | bytes 1769480 | tf_op jit(solution)/shard_map/ppermute | solution.py:26
